TPU v7x, 32 devices: a whole 2x2x4 slice. The times are simulated.
32 devices in a mesh: dev: 32 (over z, y, x, core).
Axes of the slice: x: 2, y: 2, z: 4, core: 2. Of those that a mesh axis runs over, the one named last changes fastest.
Arguments:
- tokens: bfloat16 [32768, 1024], P('dev'), may hold values from -6 to 6
- cotangent: bfloat16 [32768, 1024], P('dev'), may hold values from -6 to 6
- padding: int32 [32768], P('dev'), may hold values from 0 to 1, as said below
- image_ident: int32 [32768], P('dev'), may hold values from 0 to 48, as said below
- ln1_gain: bfloat16 [1024], P('dev'), may hold values from 0.5 to 1.5
- ln1_bias: bfloat16 [1024], P('dev'), may hold values from -3 to 3
- w_qkv: bfloat16 [1024, 3072], P('dev'), may hold values from -0.1875 to 0.1875
- b_qv: bfloat16 [2048], P('dev'), may hold values from -0.59765625 to 0.59765625
- w_out: bfloat16 [1024, 1024], P('dev'), may hold values from -2.5 to 2.5
- b_out: bfloat16 [1024], P('dev'), may hold values from -3 to 3
- ln2_gain: bfloat16 [1024], P('dev'), may hold values from 0.5 to 1.5
- ln2_bias: bfloat16 [1024], P('dev'), may hold values from -3 to 3
- w_fc: bfloat16 [4096, 1024], P('dev'), may hold values from -0.1875 to 0.1875
- b_fc: bfloat16 [4096], P('dev'), may hold values from -3 to 3
- w_proj: bfloat16 [4096, 1024], P('dev'), may hold values from -0.09375 to 0.09375
- b_proj: bfloat16 [1024], P('dev'), may hold values from -3 to 3
Outputs:
- output: bfloat16 [32768, 1024], P('dev')
- grad_tokens: bfloat16 [32768, 1024], P('dev')
- grad_ln1_gain: float32 [1024], P('dev')
- grad_ln1_bias: float32 [1024], P('dev')
- grad_w_qkv: float32 [1024, 3072], P('dev')
- grad_b_qv: float32 [2048], P('dev')
- grad_w_out: float32 [1024, 1024], P('dev')
- grad_b_out: float32 [1024], P('dev')
- grad_ln2_gain: float32 [1024], P('dev')
- grad_ln2_bias: float32 [1024], P('dev')
- grad_w_fc: float32 [4096, 1024], P('dev')
- grad_b_fc: float32 [4096], P('dev')
- grad_w_proj: float32 [4096, 1024], P('dev')
- grad_b_proj: float32 [1024], P('dev')
Inputs may be any that keep to these rules, and one draw needn't show every extreme that they name: The stream holds 49 images of exactly 577 consecutive tokens, in the order of their ids, with padding tokens between, before and after them. `image_ident`: each image's id is shared by its 577 tokens and by no other image token; a padding token carries the id of the last image before it, or 0 before the first.
All inputs are finite; a program needn't handle non-finite values.
Results may differ from a plain program's by a relative error of at most 0.012.
Values may be sent and summed in bfloat16 or wider, within the bound.
No kernel may reach another device: no remote copies, remote signals or barrier semaphores. Data moves between devices by JAX's collectives and lax.ppermute only.
A program may use at most 448 MiB of HBM per device.

v0:
```python
import jax
import jax.numpy as jnp
from jax import lax
from jax.sharding import PartitionSpec as P

HEAD_DIM = 64
IMG = 577


def with_halo(cells, sides, width):
    for axis, dim in sides:
        count = lax.axis_size(axis)
        ends = count - 1
        head = lax.slice_in_dim(cells, 0, width, axis=dim)
        tail = lax.slice_in_dim(cells, cells.shape[dim] - width, cells.shape[dim], axis=dim)
        cells = jnp.concatenate(
            [
                lax.ppermute(tail, axis, [(i, (i + 1) % count) for i in range(ends)]),
                cells,
                lax.ppermute(head, axis, [((i + 1) % count, i) for i in range(ends)]),
            ],
            axis=dim,
        )
    return cells


def shifted(value, axis, by):
    size = lax.axis_size(axis)
    pairs = [(i, i + by) for i in range(size) if 0 <= i + by < size]
    return lax.ppermute(value, axis, pairs)


def layer_norm(values, norm_gain, norm_shift):
    centered = values - jnp.mean(values, axis=-1, keepdims=True)
    spread = jnp.mean(centered * centered, axis=-1, keepdims=True)
    return centered * lax.rsqrt(spread + 1e-05) * norm_gain + norm_shift


def quick_gelu(values):
    return values * jax.nn.sigmoid(1.702 * values)


def contract_rows(matrix_one, matrix_two):
    return lax.dot_general(
        matrix_one, matrix_two, (((0,), (0,)), ((), ())), preferred_element_type=jnp.float32
    )


def contract_cols(matrix_one, matrix_two):
    return lax.dot_general(
        matrix_one, matrix_two, (((1,), (1,)), ((), ())), preferred_element_type=jnp.float32
    )


def shards(
    tokens,
    cotangent,
    padding,
    image_ident,
    ln1_gain,
    ln1_bias,
    w_qkv,
    b_qv,
    w_out,
    b_out,
    ln2_gain,
    ln2_bias,
    w_fc,
    b_fc,
    w_proj,
    b_proj,
):
    model_width = w_out.shape[1]
    tok_rows = tokens.shape[0]
    rim_rows = IMG - 1
    head_count = model_width // HEAD_DIM
    group_heads = 4
    block_rows = 512
    block_count = tok_rows // block_rows
    window_rows = block_rows + 2 * rim_rows
    score_scale = HEAD_DIM ** (-0.5)
    attn_set = (
        lax.all_gather(w_qkv, "dev", axis=0, tiled=True),
        lax.all_gather(w_out, "dev", axis=0, tiled=True),
        lax.all_gather(b_qv, "dev", axis=0, tiled=True),
        lax.all_gather(b_out, "dev", axis=0, tiled=True),
        lax.all_gather(ln1_gain, "dev", axis=0, tiled=True),
        lax.all_gather(ln1_bias, "dev", axis=0, tiled=True),
    )
    mlp_set = (
        lax.all_gather(w_fc, "dev", axis=0, tiled=True),
        lax.all_gather(w_proj, "dev", axis=0, tiled=True),
        lax.all_gather(b_fc, "dev", axis=0, tiled=True),
        lax.all_gather(b_proj, "dev", axis=0, tiled=True),
        lax.all_gather(ln2_gain, "dev", axis=0, tiled=True),
        lax.all_gather(ln2_bias, "dev", axis=0, tiled=True),
    )
    inputs_float = tokens.astype(jnp.float32)
    normed_one, ln_one_pull = jax.vjp(
        layer_norm, inputs_float, attn_set[4].astype(jnp.float32), attn_set[5].astype(jnp.float32)
    )
    normed_low = normed_one.astype(jnp.bfloat16)
    mixed_proj = jnp.dot(normed_low, attn_set[0], preferred_element_type=jnp.float32)
    bias_qv = attn_set[2].astype(jnp.float32)
    queries = (mixed_proj[:, :model_width] + bias_qv[:model_width]).astype(jnp.bfloat16)
    key_vals = jnp.concatenate(
        [
            mixed_proj[:, model_width : 2 * model_width],
            mixed_proj[:, 2 * model_width :] + bias_qv[model_width:],
        ],
        axis=1,
    ).astype(jnp.bfloat16)
    extended = with_halo(key_vals, (("dev", 0),), rim_rows)
    valid_rows = padding == 1
    places = jnp.arange(tok_rows, dtype=jnp.int32)
    same_before = jnp.concatenate(
        [jnp.zeros((1,), bool), valid_rows[:-1] & (image_ident[:-1] == image_ident[1:])]
    )
    same_after = jnp.concatenate(
        [valid_rows[1:] & (image_ident[1:] == image_ident[:-1]), jnp.zeros((1,), bool)]
    )
    run_first = lax.cummax(jnp.where(valid_rows & ~same_before, places, 0), axis=0)
    run_last = lax.cummin(
        jnp.where(valid_rows & ~same_after, places, tok_rows - 1), axis=0, reverse=True
    )
    image_first = jnp.where(run_last < tok_rows - 1, run_last - IMG + 1, run_first)
    lower_edge = jnp.where(valid_rows, image_first, places)
    upper_edge = jnp.where(valid_rows, image_first + IMG, places + 1)
    query_heads = queries.reshape(tok_rows, head_count, HEAD_DIM)

    def block_view(block_index):
        first_row = block_index * block_rows
        query_block = lax.dynamic_slice_in_dim(query_heads, first_row, block_rows, 0)
        window = lax.dynamic_slice_in_dim(extended, first_row, window_rows, 0)
        key_block = window[:, :model_width].reshape(window_rows, head_count, HEAD_DIM)
        value_block = window[:, model_width:].reshape(window_rows, head_count, HEAD_DIM)
        key_place = first_row - rim_rows + jnp.arange(window_rows, dtype=jnp.int32)
        lower_block = lax.dynamic_slice_in_dim(lower_edge, first_row, block_rows, 0)
        upper_block = lax.dynamic_slice_in_dim(upper_edge, first_row, block_rows, 0)
        key_keep = (key_place[None, :] >= lower_block[:, None]) & (
            key_place[None, :] < upper_block[:, None]
        )
        return (first_row, query_block, key_block, value_block, key_keep)

    def group_scores(query_part, key_part, key_keep):
        scores = (
            jnp.einsum("qhd,khd->hqk", query_part, key_part, preferred_element_type=jnp.float32)
            * score_scale
        )
        return jnp.where(key_keep[None], scores, -1e30)

    def attend(block_index):
        first_row, query_block, key_block, value_block, key_keep = block_view(block_index)
        pieces = []
        log_parts = []
        for group_index in range(head_count // group_heads):
            heads_slice = slice(group_index * group_heads, (group_index + 1) * group_heads)
            scores = group_scores(query_block[:, heads_slice], key_block[:, heads_slice], key_keep)
            row_peak = jnp.max(scores, axis=-1, keepdims=True)
            log_total = row_peak + jnp.log(
                jnp.sum(jnp.exp(scores - row_peak), axis=-1, keepdims=True)
            )
            soft_probs = jnp.exp(scores - log_total)
            pieces.append(
                jnp.einsum(
                    "hqk,khd->qhd",
                    soft_probs.astype(jnp.bfloat16),
                    value_block[:, heads_slice],
                    preferred_element_type=jnp.float32,
                )
            )
            log_parts.append(log_total[:, :, 0])
        mixed_heads = jnp.concatenate(pieces, axis=1).reshape(block_rows, model_width)
        return (mixed_heads.astype(jnp.bfloat16), jnp.concatenate(log_parts, axis=0))

    att_blocks, log_blocks = lax.map(attend, jnp.arange(block_count, dtype=jnp.int32))
    attended = att_blocks.reshape(tok_rows, model_width)
    branch = jnp.dot(attended, attn_set[1], preferred_element_type=jnp.float32) + attn_set[
        3
    ].astype(jnp.float32)
    middle = inputs_float + branch
    normed_two, ln_two_pull = jax.vjp(
        layer_norm, middle, mlp_set[4].astype(jnp.float32), mlp_set[5].astype(jnp.float32)
    )
    normed_two_low = normed_two.astype(jnp.bfloat16)
    hidden = contract_cols(normed_two_low, mlp_set[0]) + mlp_set[2].astype(jnp.float32)
    gelu_out, gelu_pull = jax.vjp(quick_gelu, hidden)
    gelu_low = gelu_out.astype(jnp.bfloat16)
    keep_rows = padding.astype(jnp.float32)[:, None]
    result = (
        middle
        + jnp.dot(gelu_low, mlp_set[1], preferred_element_type=jnp.float32)
        + mlp_set[3].astype(jnp.float32)
    )
    output = (keep_rows * result).astype(jnp.bfloat16)
    full_qkv, full_out = (
        lax.all_gather(w_qkv, "dev", axis=0, tiled=True),
        lax.all_gather(w_out, "dev", axis=0, tiled=True),
    )
    full_fc, full_proj = (
        lax.all_gather(w_fc, "dev", axis=0, tiled=True),
        lax.all_gather(w_proj, "dev", axis=0, tiled=True),
    )
    grad_result = keep_rows * cotangent.astype(jnp.float32)
    grad_result_low = grad_result.astype(jnp.bfloat16)
    grad_gelu = contract_cols(grad_result_low, full_proj)
    grad_hidden = gelu_pull(grad_gelu)[0].astype(jnp.bfloat16)
    grad_normed_two = jnp.dot(grad_hidden, full_fc, preferred_element_type=jnp.float32)
    grad_middle_norm, grad_gain_two, grad_shift_two = ln_two_pull(grad_normed_two)
    grad_middle = grad_result + grad_middle_norm
    grad_branch = grad_middle.astype(jnp.bfloat16)
    grad_attended = contract_cols(grad_branch, full_out).astype(jnp.bfloat16)
    grad_heads = grad_attended.reshape(tok_rows, head_count, HEAD_DIM)

    def revisit(carried, block_index):
        key_sums, value_sums = carried
        first_row, query_block, key_block, value_block, key_keep = block_view(block_index)
        grad_block = lax.dynamic_slice_in_dim(grad_heads, first_row, block_rows, 0)
        log_block = log_blocks[block_index]
        query_parts = []
        key_parts = []
        value_parts = []
        for group_index in range(head_count // group_heads):
            heads_slice = slice(group_index * group_heads, (group_index + 1) * group_heads)
            query_part = query_block[:, heads_slice]
            key_part = key_block[:, heads_slice]
            grad_part = grad_block[:, heads_slice]
            scores = group_scores(query_part, key_part, key_keep)
            soft_probs = jnp.exp(scores - log_block[heads_slice][:, :, None])
            grad_probs = jnp.einsum(
                "qhd,khd->hqk",
                grad_part,
                value_block[:, heads_slice],
                preferred_element_type=jnp.float32,
            )
            inner_sum = jnp.sum(grad_probs * soft_probs, axis=-1, keepdims=True)
            grad_scores = (soft_probs * (grad_probs - inner_sum)).astype(jnp.bfloat16)
            query_parts.append(
                jnp.einsum(
                    "hqk,khd->qhd", grad_scores, key_part, preferred_element_type=jnp.float32
                )
                * score_scale
            )
            key_parts.append(
                jnp.einsum(
                    "hqk,qhd->khd", grad_scores, query_part, preferred_element_type=jnp.float32
                )
                * score_scale
            )
            value_parts.append(
                jnp.einsum(
                    "hqk,qhd->khd",
                    soft_probs.astype(jnp.bfloat16),
                    grad_part,
                    preferred_element_type=jnp.float32,
                )
            )
        key_grad = jnp.concatenate(key_parts, axis=1).reshape(window_rows, model_width)
        value_grad = jnp.concatenate(value_parts, axis=1).reshape(window_rows, model_width)
        key_sums = lax.dynamic_update_slice_in_dim(
            key_sums,
            lax.dynamic_slice_in_dim(key_sums, first_row, window_rows, 0) + key_grad,
            first_row,
            0,
        )
        value_sums = lax.dynamic_update_slice_in_dim(
            value_sums,
            lax.dynamic_slice_in_dim(value_sums, first_row, window_rows, 0) + value_grad,
            first_row,
            0,
        )
        return (
            (key_sums, value_sums),
            jnp.concatenate(query_parts, axis=1).reshape(block_rows, model_width),
        )

    zero_sums = jnp.zeros((tok_rows + 2 * rim_rows, model_width), jnp.float32)
    (key_sums, value_sums), query_grads = lax.scan(
        revisit, (zero_sums, zero_sums), jnp.arange(block_count, dtype=jnp.int32)
    )
    grad_queries = query_grads.reshape(tok_rows, model_width).astype(jnp.bfloat16)
    to_previous = jnp.concatenate([key_sums[:rim_rows], value_sums[:rim_rows]], axis=1)
    to_following = jnp.concatenate(
        [key_sums[rim_rows + tok_rows :], value_sums[rim_rows + tok_rows :]], axis=1
    )
    from_following = shifted(to_previous.astype(jnp.bfloat16), "dev", -1).astype(to_previous.dtype)
    from_previous = shifted(to_following.astype(jnp.bfloat16), "dev", 1).astype(to_following.dtype)
    own_rows = jnp.concatenate(
        [key_sums[rim_rows : rim_rows + tok_rows], value_sums[rim_rows : rim_rows + tok_rows]],
        axis=1,
    )
    own_rows = (
        own_rows.at[:rim_rows].add(from_previous).at[tok_rows - rim_rows :].add(from_following)
    )
    grad_kv = own_rows.astype(jnp.bfloat16)
    grad_mixed = jnp.concatenate([grad_queries, grad_kv], axis=1)
    grad_normed_one = contract_cols(grad_mixed, full_qkv)
    grad_inner, grad_gain_one, grad_shift_one = ln_one_pull(grad_normed_one)
    grad_tokens = (grad_middle + grad_inner).astype(jnp.bfloat16)
    attn_grads = lax.psum_scatter(
        jnp.concatenate(
            [contract_rows(normed_low, grad_mixed), contract_rows(attended, grad_branch)], axis=1
        ),
        "dev",
        scatter_dimension=0,
        tiled=True,
    )
    mlp_grads = lax.psum_scatter(
        jnp.concatenate(
            [contract_rows(grad_hidden, normed_two_low), contract_rows(gelu_low, grad_result_low)],
            axis=1,
        ),
        "dev",
        scatter_dimension=0,
        tiled=True,
    )
    bias_qv_grad = jnp.concatenate(
        [
            jnp.sum(grad_queries.astype(jnp.float32), axis=0),
            jnp.sum(grad_kv[:, model_width:].astype(jnp.float32), axis=0),
        ]
    )
    small_sums = (
        lax.psum_scatter(bias_qv_grad, "dev", scatter_dimension=0, tiled=True),
        lax.psum_scatter(
            jnp.sum(grad_branch.astype(jnp.float32), axis=0), "dev", scatter_dimension=0, tiled=True
        ),
        lax.psum_scatter(grad_gain_one, "dev", scatter_dimension=0, tiled=True),
        lax.psum_scatter(grad_shift_one, "dev", scatter_dimension=0, tiled=True),
        lax.psum_scatter(
            jnp.sum(grad_hidden.astype(jnp.float32), axis=0), "dev", scatter_dimension=0, tiled=True
        ),
        lax.psum_scatter(jnp.sum(grad_result, axis=0), "dev", scatter_dimension=0, tiled=True),
        lax.psum_scatter(grad_gain_two, "dev", scatter_dimension=0, tiled=True),
        lax.psum_scatter(grad_shift_two, "dev", scatter_dimension=0, tiled=True),
    )
    return (
        output,
        grad_tokens,
        small_sums[2],
        small_sums[3],
        attn_grads[:, : 3 * model_width],
        small_sums[0],
        attn_grads[:, 3 * model_width :],
        small_sums[1],
        small_sums[6],
        small_sums[7],
        mlp_grads[:, :model_width],
        small_sums[4],
        mlp_grads[:, model_width:],
        small_sums[5],
    )


def solution(mesh):
    return jax.shard_map(
        shards,
        mesh=mesh,
        in_specs=(
            P("dev", None),
            P("dev", None),
            P("dev"),
            P("dev"),
            P("dev"),
            P("dev"),
            P("dev", None),
            P("dev"),
            P("dev", None),
            P("dev"),
            P("dev"),
            P("dev"),
            P("dev", None),
            P("dev"),
            P("dev", None),
            P("dev"),
        ),
        out_specs=(
            P("dev", None),
            P("dev", None),
            P("dev"),
            P("dev"),
            P("dev", None),
            P("dev"),
            P("dev", None),
            P("dev"),
            P("dev"),
            P("dev"),
            P("dev", None),
            P("dev"),
            P("dev", None),
            P("dev"),
        ),
        check_vma=False,
    )
```

profile of v0, /device:TPU:0, one launch (start us, length us, event | category | flops | bytes accessed | tf_op | source)
XLA Modules:
  0.0 1727.4 jit_solution(1058867059143225031)
XLA Ops:
  15.3 42.6 %all-reduce.16 = (bf16[2048]{0:T(1024)(128)(2,1)S(1)}, bf16[1024]{0:T(1024)(128)(2,1)S(1)}, bf16[1024]{0:T(1024)(128)(2,1)S(1)}, bf16[1024]{0:T(1024)(128)(2,1)S...) all-reduce(bf16[2048]{0:T(1024)(128)(2,1)S(1)} %dynamic-update-slic, ...), channel_id=1, replica_groups=mesh['dev'=32] {'dev'}, use_global_device_ids=true, to_apply=%add.2 | all-reduce | flops 8192 | bytes 32768
  62.4 20.5 %all-gather.6.cloned.1.call-done = bf16[1024,3072]{1,0:T(8,128)(2,1)} async-done(((bf16[32,3072]{1,0:T(8,128)(2,1)}), bf16[1024,3072]{1,0:T(8,128)(2,1)}) %all-gather.6.cloned.1.call-update) | async-done | bytes 6291472 | tf_op jit(solution)/shard_map/all_gather | solution.py:83
  116.2 77.9 %all-gather = bf16[32,1,128]{2,1,0:T(2,128)(2,1)S(1)} all-gather(bf16[1,1,128]{2,1,0:T(2,128)(2,1)S(1)} %bitcast.236), channel_id=1, replica_groups=mesh['dev'=32] {'dev'}, dimensions={0}, use_global_device_ids=true | all-gather | bytes 8448 | tf_op jit(solution)/shard_map/all_gather | solution.py:93
  218.6 219.9 %while.32 = (s32[]{:T(128)}, bf16[2,512,1024]{2,1,0:T(8,128)(2,1)}, f32[2,16,512]{2,1,0:T(8,128)}, s32[2]{0:T(128)S(1)}, bf16[2176,2048]{0,1:T(8,128)(2,1)}, /*i...) while((s32[]{:T(128)}, bf16[2,512,1024]{2,1,0:T(8,128)(2,1)}, ...), condition=%wide.region_15.16_spmd, body=%wide.region_6.15_spmd.sunk | while | flops 3644278272 | bytes 309914080 | solution.py:176
  263.7 21.5 %exponential_reduce_fusion.6 = (f32[4,512]{1,0:T(4,128)S(1)}, f32[4,512]{1,0:T(4,128)S(1)}, f32[4,512]{1,0:T(4,128)S(1)}, f32[4,512]{1,0:T(4,128)S(1)}, f32[4,512,1664]{2,1,0:T(8,128)}) fusion(f32[4,512,1664]{2,1,0:T(8,128)} %get-tuple-element.647, f32[4,512]{1,0:T(4,128)S(1)} %get-tuple-element.648, pred[512,1664]{1,0:T(8,128)(4,1)} %compare_and_fusion.6, ...), kind=kOutput, calls=%fused_computation.10.clone.1 | convolution fusion | flops 480501760 | bytes 57319428 | tf_op jit(solution)/shard_map/while/body/eval_jaxpr/qhd,khd->hqk/dot_general | solution.py:147
  285.1 17.5 %exponential_reduce_fusion.7 = (f32[4,512]{1,0:T(4,128)S(1)}, f32[4,512]{1,0:T(4,128)S(1)}, f32[4,512]{1,0:T(4,128)S(1)}) fusion(f32[4,512,1664]{2,1,0:T(8,128)} %get-tuple-element.650, f32[4,512]{1,0:T(4,128)S(1)} %get-tuple-element.651, pred[512,1664]{1,0:T(8,128)(4,1)} %compare_and_fusion.6, f32[4,512]{1,0:T(4,128)S(1)} %get-tuple-element.652, ...), kind=kLoop, calls=%fused_computation.7.clone.1 | loop fusion | flops 40888320 | bytes 41795584 | tf_op jit(solution)/shard_map/while/body/eval_jaxpr/reduce_sum | solution.py:161
  361.3 21.1 %exponential_reduce_fusion.6 = (f32[4,512]{1,0:T(4,128)S(1)}, f32[4,512]{1,0:T(4,128)S(1)}, f32[4,512]{1,0:T(4,128)S(1)}, f32[4,512]{1,0:T(4,128)S(1)}, f32[4,512,1664]{2,1,0:T(8,128)}) fusion(f32[4,512,1664]{2,1,0:T(8,128)} %get-tuple-element.647, f32[4,512]{1,0:T(4,128)S(1)} %get-tuple-element.648, pred[512,1664]{1,0:T(8,128)(4,1)} %compare_and_fusion.6, ...), kind=kOutput, calls=%fused_computation.10.clone.1 | convolution fusion | flops 480501760 | bytes 57319428 | tf_op jit(solution)/shard_map/while/body/eval_jaxpr/qhd,khd->hqk/dot_general | solution.py:147
  382.4 16.3 exponential_reduce_fusion.7
  446.8 17.2 fusion.180
  464.1 22.1 %convert_reduce_fusion = (f32[4096]{0:T(1024)}, bf16[1024,4096]{1,0:T(8,128)(2,1)}) fusion(f32[1024,4096]{1,0:T(8,128)} %fusion.180, f32[4096]{0:T(1024)S(1)} %bitcast.233, bf16[4096,1024]{1,0:T(8,128)(2,1)} %all-gather.12.cloned.1.call-done, bf16[1024,1024]{0,1:T(8,128)(2,1)S(1)} %copy-done.16, f32[1024]{0:T(1024)S(1)} %copy-done.47), kind=kOutput, calls=%fused_computation.191 | convolution fusion | flops 8655990784 | bytes 35688448 | tf_op jit(solution)/shard_map/dot_general | solution.py:50
  486.2 15.9 fusion.190
  530.5 559.2 %while.33 = (s32[]{:T(128)}, f32[2176,1024]{1,0:T(8,128)}, f32[2176,1024]{1,0:T(8,128)}, bf16[2,512,1024]{2,1,0:T(8,128)(2,1)}, s32[2]{0:T(128)S(1)}, /*index=5*...) while((s32[]{:T(128)}, f32[2176,1024]{1,0:T(8,128)}, ...), condition=%wide.region_25.26_spmd, body=%wide.region_20.25_spmd.sunk | while | flops 8949131264 | bytes 932702528 | solution.py:278
  587.8 38.3 %multiply_reduce_fusion.8 = (f32[4,512]{1,0:T(4,128)S(1)}, f32[4,512]{1,0:T(4,128)S(1)}, f32[4,512]{1,0:T(4,128)S(1)}, f32[4,512]{1,0:T(4,128)S(1)}, f32[4,512,1664]{2,1,0:T(8,128)}) fusion(f32[4,512,1664]{2,1,0:T(8,128)} %fusion.355, f32[4,512]{1,0:T(4,128)S(1)} %get-tuple-element.676, pred[512,1664]{1,0:T(8,128)(4,1)} %compare_and_fusion.7, ...), kind=kOutput, calls=%fused_computation.77.clone.1 | convolution fusion | flops 504356864 | bytes 111869952 | tf_op jit(solution)/shard_map/while/body/eval_jaxpr/qhd,khd->hqk/dot_general | solution.py:230
  626.1 46.2 %multiply_convert_fusion.9 = (bf16[4,512,1664]{2,1,0:T(8,128)(2,1)}, bf16[4,512,1664]{2,1,0:T(8,128)(2,1)}, bf16[4,512,1664]{2,1,0:T(8,128)(2,1)}, bf16[4,512,1664]{2,1,0:T(8,128)(2,1)}) fusion(f32[4,512,1664]{2,1,0:T(8,128)} %get-tuple-element.678, f32[4,512,1664]{2,1,0:T(8,128)} %fusion.355, f32[4,512]{1,0:T(4,128)S(1)} %get-tuple-element.679, ...), kind=kLoop, calls=%fused_computation.76.clone.1 | loop fusion | flops 81788928 | bytes 137232384 | tf_op jit(solution)/shard_map/while/body/eval_jaxpr/convert_element_type | solution.py:237
  862.6 38.3 %multiply_reduce_fusion.8 = (f32[4,512]{1,0:T(4,128)S(1)}, f32[4,512]{1,0:T(4,128)S(1)}, f32[4,512]{1,0:T(4,128)S(1)}, f32[4,512]{1,0:T(4,128)S(1)}, f32[4,512,1664]{2,1,0:T(8,128)}) fusion(f32[4,512,1664]{2,1,0:T(8,128)} %fusion.355, f32[4,512]{1,0:T(4,128)S(1)} %get-tuple-element.676, pred[512,1664]{1,0:T(8,128)(4,1)} %compare_and_fusion.7, ...), kind=kOutput, calls=%fused_computation.77.clone.1 | convolution fusion | flops 504356864 | bytes 111869952 | tf_op jit(solution)/shard_map/while/body/eval_jaxpr/qhd,khd->hqk/dot_general | solution.py:230
  900.9 46.4 %multiply_convert_fusion.9 = (bf16[4,512,1664]{2,1,0:T(8,128)(2,1)}, bf16[4,512,1664]{2,1,0:T(8,128)(2,1)}, bf16[4,512,1664]{2,1,0:T(8,128)(2,1)}, bf16[4,512,1664]{2,1,0:T(8,128)(2,1)}) fusion(f32[4,512,1664]{2,1,0:T(8,128)} %get-tuple-element.678, f32[4,512,1664]{2,1,0:T(8,128)} %fusion.355, f32[4,512]{1,0:T(4,128)S(1)} %get-tuple-element.679, ...), kind=kLoop, calls=%fused_computation.76.clone.1 | loop fusion | flops 81788928 | bytes 137232384 | tf_op jit(solution)/shard_map/while/body/eval_jaxpr/convert_element_type | solution.py:237
  1067.5 12.8 constant_dynamic-update-slice_fusion.8
  1144.6 16.7 fusion.179
  1161.3 15.9 fusion.164
  1177.2 23.3 %pad_maximum_fusion.4 = f32[4096,2048]{0,1:T(8,128)} fusion(f32[4096,1024]{0,1:T(8,128)} %fusion.164, f32[4096,1024]{0,1:T(8,128)} %fusion.179), kind=kLoop, calls=%fused_computation.184 | loop fusion | flops 8388608 | bytes 67108864 | tf_op jit(solution)/shard_map/concatenate | solution.py:309
  1201.2 17.2 multiply_convert_fusion.5
  1252.0 73.4 %all-reduce.15 = (f32[1024]{0:T(1024)S(1)}, f32[1024]{0:T(1024)S(1)}, f32[2048]{0:T(1024)S(1)}, f32[1024]{0:T(1024)S(1)}, f32[1024]{0:T(1024)S(1)}, /*index=5*/f...) all-reduce(f32[1024]{0:T(1024)S(1)} %get-tuple-element.396, ...), channel_id=2, replica_groups=mesh['dev'=32] {'dev'}, use_global_device_ids=true, to_apply=%region_29.30.clone | all-reduce | flops 12288 | bytes 98304
  1334.0 24.9 %reduce-scatter.3.cloned.1.call-done = f32[32,4096]{1,0:T(8,128)} async-done(((f32[1024,4096]{1,0:T(8,128)}), f32[32,4096]{1,0:T(8,128)}) %reduce-scatter.3.cloned.1.call-update) | async-done | bytes 524304 | tf_op jit(solution)/shard_map/reduce_scatter | solution.py:300
  1362.2 354.9 %reduce-scatter.5.cloned.1.call-done = f32[128,2048]{0,1:T(8,128)} async-done(((f32[4096,2048]{0,1:T(8,128)}), f32[128,2048]{0,1:T(8,128)}) %reduce-scatter.5.cloned.1.call-update) | async-done | bytes 1048592 | tf_op jit(solution)/shard_map/reduce_scatter | solution.py:308
  (525 shorter events, 687.6 us)
Async XLA Ops:
  7.2 75.7 %all-gather.6.cloned.1.call-start = ((), (), s32[]{:S(2)}) async-start(), calls=%async_computation.2 | async-start | bytes 6488064 | tf_op jit(solution)/shard_map/all_gather | solution.py:83
  7.9 430.6 %all-gather.8.cloned.1.call-start = ((), (), s32[]{:S(2)}) async-start(), calls=%async_computation.3 | async-start | bytes 2162688 | tf_op jit(solution)/shard_map/all_gather | solution.py:84
  8.7 438.1 %all-gather.10.cloned.1.call-start = ((), (), s32[]{:S(2)}) async-start(), calls=%async_computation.4 | async-start | bytes 8650752 | tf_op jit(solution)/shard_map/all_gather | solution.py:91
  9.4 454.7 %all-gather.12.cloned.1.call-start = ((), (), s32[]{:S(2)}) async-start(), calls=%async_computation.5 | async-start | bytes 8650752 | tf_op jit(solution)/shard_map/all_gather | solution.py:92
  57.9 34.3 %copy-start.39 = (f32[1024]{0:T(1024)}, f32[1024]{0:T(1024)S(1)}, u32[]{:S(2)}) copy-start(f32[1024]{0:T(1024)S(1)} %convert_element_type.183) | copy-start | bytes 12292
  57.9 34.3 %copy-start.64 = (f32[1024]{0:T(1024)}, f32[1024]{0:T(1024)S(1)}, u32[]{:S(2)}) copy-start(f32[1024]{0:T(1024)S(1)} %convert_element_type.184) | copy-start | bytes 12292
  60.8 31.4 %copy-start.6 = (bf16[1024,1024]{0,1:T(8,128)(2,1)}, bf16[1024,1024]{0,1:T(8,128)(2,1)S(1)}, u32[]{:S(2)}) copy-start(bf16[1024,1024]{0,1:T(8,128)(2,1)S(1)} %copy.64) | copy-start | bytes 6291460
  61.2 31.0 %copy-start.35 = (f32[1024]{0:T(1024)}, f32[1024]{0:T(1024)S(1)}, u32[]{:S(2)}) copy-start(f32[1024]{0:T(1024)S(1)} %broadcast_multiply_fusion.1) | copy-start | bytes 12292
  62.4 29.8 %copy-start.44 = (f32[1024]{0:T(1024)}, f32[1024]{0:T(1024)S(1)}, u32[]{:S(2)}) copy-start(f32[1024]{0:T(1024)S(1)} %fusion.172) | copy-start | bytes 12292
  95.2 21.0 %copy-start.70 = (bf16[128]{0:T(256)(128)(2,1)S(1)}, bf16[128]{0:T(256)(128)(2,1)}, u32[]{:S(2)}) copy-start(bf16[128]{0:T(256)(128)(2,1)} %param.37) | copy-start | bytes 772
  101.5 97.4 %copy-start.20 = (bf16[1024,1024]{1,0:T(8,128)(2,1)S(1)}, bf16[1024,1024]{1,0:T(8,128)(2,1)}, u32[]{:S(2)}) copy-start(bf16[1024,1024]{1,0:T(8,128)(2,1)} %copy-done.19) | copy-start | bytes 6291460
  101.5 97.4 %collective-permute-start = (bf16[576,2048]{1,0:T(8,128)(2,1)}, bf16[576,2048]{1,0:T(8,128)(2,1)}, u32[]{:S(2)}, u32[]{:S(2)}) collective-permute-start(bf16[576,2048]{1,0:T(8,128)(2,1)} %get-tuple-element.485), channel_id=1, source_target_pairs={{0,1},{1,2},{2,3},{3,4},{4,5},{5,6},{6,7},{7,8},{8,9},{9,10},{10,1... | collective-permute-start | bytes 7077896 | tf_op jit(solution)/shard_map/ppermute | solution.py:18
  105.2 93.7 %collective-permute-start.1 = (bf16[576,2048]{1,0:T(8,128)(2,1)}, bf16[576,2048]{1,0:T(8,128)(2,1)}, u32[]{:S(2)}, u32[]{:S(2)}) collective-permute-start(bf16[576,2048]{1,0:T(8,128)(2,1)} %get-tuple-element.486), channel_id=1, source_target_pairs={{1,0},{2,1},{3,2},{4,3},{5,4},{6,5},{7,6},{8,7},{9,8},{10,9},{11,1... | collective-permute-start | bytes 7077896 | tf_op jit(solution)/shard_map/ppermute | solution.py:20
  106.5 1252.3 %reduce-scatter.3.cloned.1.call-start = ((), (), s32[]{:S(2)}) async-start(), calls=%async_computation.6 | async-start | bytes 17301504 | tf_op jit(solution)/shard_map/reduce_scatter | solution.py:300
  218.6 219.9 %copy-start.68 = (f32[1024]{0:T(1024)S(1)}, f32[1024]{0:T(1024)}, u32[]{:S(2)}) copy-start(f32[1024]{0:T(1024)} %convert_element_type.188) | copy-start | bytes 12292
  285.1 18.1 %copy-start.5 = (pred[512,1664]{1,0:T(8,128)(4,1)S(1)}, pred[512,1664]{1,0:T(8,128)(4,1)}, u32[]{:S(2)}) copy-start(pred[512,1664]{1,0:T(8,128)(4,1)} %compare_and_fusion.6) | copy-start | bytes 2555908 | tf_op jit(solution)/shard_map/while
  444.2 68.7 %copy-start.42 = (f32[1024]{0:T(1024)}, f32[1024]{0:T(1024)S(1)}, u32[]{:S(2)}) copy-start(f32[1024]{0:T(1024)S(1)} %broadcast_multiply_fusion) | copy-start | bytes 12292
  446.7 66.1 %copy-start.53 = (f32[1024]{0:T(1024)}, f32[1024]{0:T(1024)S(1)}, u32[]{:S(2)}) copy-start(f32[1024]{0:T(1024)S(1)} %fusion.173) | copy-start | bytes 12292
  537.7 41.3 %copy-start.2 = (bf16[1664,1024]{0,1:T(8,128)(2,1)}, bf16[1664,1024]{0,1:T(8,128)(2,1)S(1)}, u32[]{:S(2)}) copy-start(bf16[1664,1024]{0,1:T(8,128)(2,1)S(1)} %get-tuple-element.677) | copy-start | bytes 10223620 | tf_op jit(solution)/shard_map/while
  812.5 41.4 %copy-start.2 = (bf16[1664,1024]{0,1:T(8,128)(2,1)}, bf16[1664,1024]{0,1:T(8,128)(2,1)S(1)}, u32[]{:S(2)}) copy-start(bf16[1664,1024]{0,1:T(8,128)(2,1)S(1)} %get-tuple-element.677) | copy-start | bytes 10223620 | tf_op jit(solution)/shard_map/while
  1098.3 21.5 %collective-permute-start.2 = (bf16[576,2048]{1,0:T(8,128)(2,1)}, bf16[576,2048]{1,0:T(8,128)(2,1)}, u32[]{:S(2)}, u32[]{:S(2)}) collective-permute-start(bf16[576,2048]{1,0:T(8,128)(2,1)} %pad_maximum_fusion.12), channel_id=1, source_target_pairs={{0,1},{1,2},{2,3},{3,4},{4,5},{5,6},{6,7},{7,8},{8,9},{9,10},{10,1... | collective-permute-start | bytes 7077896 | tf_op jit(solution)/shard_map/ppermute | solution.py:30
  1103.7 18.6 %collective-permute-start.3 = (bf16[576,2048]{1,0:T(8,128)(2,1)}, bf16[576,2048]{1,0:T(8,128)(2,1)}, u32[]{:S(2)}, u32[]{:S(2)}) collective-permute-start(bf16[576,2048]{1,0:T(8,128)(2,1)} %pad_maximum_fusion.13), channel_id=1, source_target_pairs={{1,0},{2,1},{3,2},{4,3},{5,4},{6,5},{7,6},{8,7},{9,8},{10,9},{11,1... | collective-permute-start | bytes 7077896 | tf_op jit(solution)/shard_map/ppermute | solution.py:30
  1143.9 17.4 %copy-start.17 = (bf16[1024,1024]{0,1:T(8,128)(2,1)S(1)}, bf16[1024,1024]{0,1:T(8,128)(2,1)}, u32[]{:S(2)}) copy-start(bf16[1024,1024]{0,1:T(8,128)(2,1)} %copy.69) | copy-start | bytes 6291460
  1144.0 573.1 %reduce-scatter.5.cloned.1.call-start = ((), (), s32[]{:S(2)}) async-start(), calls=%async_computation.7 | async-start | bytes 34603008 | tf_op jit(solution)/shard_map/reduce_scatter | solution.py:308
  (119 other events, 845.8 us)
Sparse Core Ops, SparseCore 0:
  10.8 71.9 all-gather.5
  85.7 76.4 all-gather.7
  165.1 75.8 all-gather.9
  243.7 75.6 all-gather.11
  1144.0 214.7 reduce-scatter.2
  1361.0 356.0 reduce-scatter.4
where the time goes:
time: 1740 us; the launch traced here: 1730 us
  matrix products  566 us (33%)
  waiting for transfers between devices  402 us (23%)
  other arithmetic  276 us (16%)
  local copies, waits for them, and re-layouts  219 us (13%)
  blocking collectives  194 us (11%)
  loops' own time  44 us (3%)
    reduce_scatter x1, waiting for transfers between devices, shards(): lax.psum_scatter(jnp.concatenate([contract_rows(grad_hidden, normed_two_l...  355 us
    dot_general x16, matrix products, group_scores(): jnp.einsum('qhd,khd->hqk', query_part, key_part, preferred_element_type=j...  138 us
    dot_general x8, matrix products, revisit(): jnp.einsum('qhd,khd->hqk', grad_part, value_block[:, heads_slice], prefer...  118 us
    unnamed x2, blocking collectives  116 us
    convert_element_type x2, other arithmetic, revisit(): grad_scores = (soft_probs * (grad_probs - inner_sum)).astype(jnp.bfloat16)  92.5 us
    all_gather x1, blocking collectives, shards(): lax.all_gather(b_fc, 'dev', axis=0, tiled=True)  77.9 us
    dot_general x8, matrix products, attend(): jnp.einsum('hqk,khd->qhd', soft_probs.astype(jnp.bfloat16), value_block[:...  57.9 us
    dot_general x4, matrix products, contract_cols(): lax.dot_general(matrix_one, matrix_two, (((1,), (1,)), ((), ())), preferr...  54.6 us
  transfers between devices with their start and end apart: 10, of which 3 were waited for; matrix products, arithmetic and copies ran while one was open for 24% of the time, Pallas kernels for 0%

commit v1 on v0

v1 whole, which is shorter than its diff:
```python
import jax
import jax.numpy as jnp
from jax import lax
from jax.experimental import pallas as pl
from jax.experimental.pallas import tpu as pltpu
from jax.sharding import PartitionSpec as P

HEAD_DIM = 64
IMG = 577
RIM = IMG - 1
TILE = 128
KEYS = 592
LANES = 256
MASKED = -1e30
NOWHERE = 1 << 20


def dot_nt(a, b):
    return lax.dot_general(a, b, (((1,), (1,)), ((), ())), preferred_element_type=jnp.float32)


def dot_tn(a, b):
    return lax.dot_general(a, b, (((0,), (0,)), ((), ())), preferred_element_type=jnp.float32)


def dot_nn(a, b):
    return lax.dot_general(a, b, (((1,), (0,)), ((), ())), preferred_element_type=jnp.float32)


def paired(block):
    first = lax.broadcasted_iota(jnp.int32, block.shape, 1) < HEAD_DIM
    none = jnp.zeros_like(block)
    return jnp.concatenate([jnp.where(first, block, none), jnp.where(first, none, block)], axis=0)


def unpaired(wide):
    both = jnp.concatenate([wide[:HEAD_DIM, :TILE], wide[HEAD_DIM:, TILE:]], axis=0)
    return both.T


def key_window(first, ext_rows):
    low = first + RIM
    start = jnp.clip((low // 16) * 16, 0, ext_rows - KEYS)
    return pl.multiple_of(start, 16), low - start


def keep_image(scores, offset):
    edge = lax.broadcasted_iota(jnp.int32, (16, scores.shape[1]), 0)
    top = jnp.where(edge >= offset, scores[:16], MASKED)
    low = jnp.where(edge + (KEYS - 16) < offset + IMG, scores[KEYS - 16 :], MASKED)
    return jnp.concatenate([top, scores[16 : KEYS - 16], low], axis=0)


def attend_body(first_ref, q_ref, k_ref, v_ref, out_ref, lse_ref):
    rows = q_ref.shape[0]
    tiles = rows // TILE

    def tile(j, carry):
        at = pl.multiple_of(j * TILE, TILE)
        here = pl.ds(at, TILE)

        def item(first, pair):
            lanes = slice(pair * 128, pair * 128 + 128)
            start, offset = key_window(first, k_ref.shape[0])
            scores = dot_nt(k_ref[pl.ds(start, KEYS), lanes], paired(q_ref[here, lanes]))
            scores = keep_image(scores, offset)
            peak = jnp.max(scores, axis=0, keepdims=True)
            weights = jnp.exp(scores - peak)
            total = jnp.sum(weights, axis=0, keepdims=True)
            mixed = dot_tn(v_ref[pl.ds(start, KEYS), lanes], weights.astype(jnp.bfloat16))
            mixed = unpaired(mixed / total)
            row = lax.broadcasted_iota(jnp.int32, (TILE, 128), 0) + at
            inside = (row >= first) & (row < first + IMG)
            return jnp.where(inside, mixed, 0.0).astype(jnp.bfloat16), peak + jnp.log(total)

        one, two = first_ref[j], first_ref[tiles + j]
        for pair in range(LANES // 128):
            mixed, lse = item(one, pair)
            out_ref[here, pair * 128 : pair * 128 + 128] = mixed
            lse_ref[0, 2 * pair : 2 * pair + 1, here] = lse[:, :TILE]
            lse_ref[0, 2 * pair + 1 : 2 * pair + 2, here] = lse[:, TILE:]

        @pl.when(two != one)
        def _():
            column = lax.broadcasted_iota(jnp.int32, (1, TILE), 1) + at
            inside = (column >= two) & (column < two + IMG)
            for pair in range(LANES // 128):
                lanes = slice(pair * 128, pair * 128 + 128)
                mixed, lse = item(two, pair)
                out_ref[here, lanes] = out_ref[here, lanes] + mixed
                for head in range(2):
                    line = slice(2 * pair + head, 2 * pair + head + 1)
                    new = lse[:, head * TILE : head * TILE + TILE]
                    lse_ref[0, line, here] = jnp.where(inside, new, lse_ref[0, line, here])

        return carry

    lax.fori_loop(0, tiles, tile, 0)


def attend_back_body(
    first_ref, q_ref, k_ref, v_ref, grad_ref, lse_ref, dq_ref, dk_ref, dv_ref, dk_sum, dv_sum
):
    rows = q_ref.shape[0]
    tiles = rows // TILE
    dk_sum[...] = jnp.zeros_like(dk_sum)
    dv_sum[...] = jnp.zeros_like(dv_sum)

    def tile(j, carry):
        at = pl.multiple_of(j * TILE, TILE)
        here = pl.ds(at, TILE)
        column = lax.broadcasted_iota(jnp.int32, (1, TILE), 1) + at

        def item(first, pair):
            lanes = slice(pair * 128, pair * 128 + 128)
            start, offset = key_window(first, k_ref.shape[0])
            window = pl.ds(start, KEYS)
            keys = k_ref[window, lanes]
            queries = paired(q_ref[here, lanes])
            grads = paired(grad_ref[here, lanes])
            inside = (column >= first) & (column < first + IMG)
            lse = jnp.concatenate(
                [
                    jnp.where(inside, lse_ref[0, 2 * pair : 2 * pair + 1, here], -MASKED),
                    jnp.where(inside, lse_ref[0, 2 * pair + 1 : 2 * pair + 2, here], -MASKED),
                ],
                axis=1,
            )
            probs = jnp.exp(keep_image(dot_nt(keys, queries), offset) - lse)
            grad_probs = dot_nt(v_ref[window, lanes], grads)
            dv_sum[window, lanes] += dot_nn(probs.astype(jnp.bfloat16), grads)
            inner = jnp.sum(grad_probs * probs, axis=0, keepdims=True)
            grad_scores = (probs * (grad_probs - inner)).astype(jnp.bfloat16)
            dk_sum[window, lanes] += dot_nn(grad_scores, queries)
            return unpaired(dot_tn(keys, grad_scores) * HEAD_DIM**-0.5).astype(jnp.bfloat16)

        one, two = first_ref[j], first_ref[tiles + j]
        for pair in range(LANES // 128):
            dq_ref[here, pair * 128 : pair * 128 + 128] = item(one, pair)

        @pl.when(two != one)
        def _():
            for pair in range(LANES // 128):
                lanes = slice(pair * 128, pair * 128 + 128)
                dq_ref[here, lanes] = dq_ref[here, lanes] + item(two, pair)

        return carry

    lax.fori_loop(0, tiles, tile, 0)
    dk_ref[...] = dk_sum[...].astype(jnp.bfloat16)
    dv_ref[...] = dv_sum[...].astype(jnp.bfloat16)


def attention_cost(rows, width, products):
    return pl.CostEstimate(
        flops=2 * products * 10 * TILE * KEYS * width,
        bytes_accessed=16 * rows * width,
        transcendentals=10 * TILE * KEYS * (width // HEAD_DIM),
    )


def attend(firsts, queries, key_vals):
    rows, width = queries.shape
    ext = key_vals.shape[0]
    groups = width // LANES
    return pl.pallas_call(
        attend_body,
        grid_spec=pltpu.PrefetchScalarGridSpec(
            num_scalar_prefetch=1,
            grid=(groups,),
            in_specs=[
                pl.BlockSpec((rows, LANES), lambda g, f: (0, g)),
                pl.BlockSpec((ext, LANES), lambda g, f: (0, g)),
                pl.BlockSpec((ext, LANES), lambda g, f: (0, g + groups)),
            ],
            out_specs=[
                pl.BlockSpec((rows, LANES), lambda g, f: (0, g)),
                pl.BlockSpec((1, LANES // HEAD_DIM, rows), lambda g, f: (g, 0, 0)),
            ],
        ),
        out_shape=[
            jax.ShapeDtypeStruct((rows, width), jnp.bfloat16),
            jax.ShapeDtypeStruct((groups, LANES // HEAD_DIM, rows), jnp.float32),
        ],
        cost_estimate=attention_cost(rows, width, 2),
        name="attend",
    )(firsts, queries, key_vals, key_vals)


def attend_back(firsts, queries, key_vals, grads, lse):
    rows, width = queries.shape
    ext = key_vals.shape[0]
    groups = width // LANES
    own = pl.BlockSpec((rows, LANES), lambda g, f: (0, g))
    wide = pl.BlockSpec((ext, LANES), lambda g, f: (0, g))
    return pl.pallas_call(
        attend_back_body,
        grid_spec=pltpu.PrefetchScalarGridSpec(
            num_scalar_prefetch=1,
            grid=(groups,),
            in_specs=[
                own,
                wide,
                pl.BlockSpec((ext, LANES), lambda g, f: (0, g + groups)),
                own,
                pl.BlockSpec((1, LANES // HEAD_DIM, rows), lambda g, f: (g, 0, 0)),
            ],
            out_specs=[own, wide, wide],
            scratch_shapes=[pltpu.VMEM((ext, LANES), jnp.float32)] * 2,
        ),
        out_shape=[
            jax.ShapeDtypeStruct((rows, width), jnp.bfloat16),
            jax.ShapeDtypeStruct((ext, width), jnp.bfloat16),
            jax.ShapeDtypeStruct((ext, width), jnp.bfloat16),
        ],
        cost_estimate=attention_cost(rows, width, 5),
        name="attend_back",
    )(firsts, queries, key_vals, key_vals, grads, lse)


def image_firsts(padding, ident):
    rows = padding.shape[0]
    tiles = rows // TILE
    real = padding == 1
    by_tile = jnp.where(real, ident, NOWHERE).reshape(tiles, TILE)
    low_id = jnp.min(by_tile, axis=1)
    high_id = jnp.max(jnp.where(real, ident, -1).reshape(tiles, TILE), axis=1)
    wanted = jnp.concatenate([low_id, high_id])
    place = jnp.arange(rows, dtype=jnp.int32)[None, :]
    mine = real[None, :] & (ident[None, :] == wanted[:, None])
    run_first = jnp.min(jnp.where(mine, place, NOWHERE), axis=1)
    run_last = jnp.max(jnp.where(mine, place, -1), axis=1)
    firsts = jnp.where(run_last < rows - 1, run_last - RIM, run_first)
    empty = jnp.concatenate([low_id, low_id]) == NOWHERE
    before = jnp.tile(jnp.arange(tiles, dtype=jnp.int32) * TILE - IMG, 2)
    return jnp.where(empty, before, firsts)


def normed_parts(values):
    centered = values - jnp.mean(values, axis=-1, keepdims=True)
    spread = jnp.mean(centered * centered, axis=-1, keepdims=True)
    scale = lax.rsqrt(spread + 1e-05)
    return centered * scale, scale


def norm_back(unit, scale, gain, grads):
    scaled = grads * gain
    return scale * (
        scaled
        - jnp.mean(scaled, axis=-1, keepdims=True)
        - unit * jnp.mean(scaled * unit, axis=-1, keepdims=True)
    )


def quick_gelu(values):
    return values * jax.nn.sigmoid(1.702 * values)


def shifted(value, by):
    size = lax.axis_size("dev")
    pairs = [(i, i + by) for i in range(size) if 0 <= i + by < size]
    return lax.ppermute(value, "dev", pairs)


def shards(
    tokens,
    cotangent,
    padding,
    image_ident,
    ln1_gain,
    ln1_bias,
    w_qkv,
    b_qv,
    w_out,
    b_out,
    ln2_gain,
    ln2_bias,
    w_fc,
    b_fc,
    w_proj,
    b_proj,
):
    low = jnp.bfloat16
    wide = jnp.float32
    size = lax.axis_size("dev")
    width = w_out.shape[1]
    rows = tokens.shape[0]
    feat_rows = w_qkv.shape[0]
    smalls = (ln1_gain, ln1_bias, b_qv, b_out, ln2_gain, ln2_bias, b_fc, b_proj)
    small_all = jnp.concatenate(smalls)
    extra = 128 * -(-small_all.shape[0] // (128 * feat_rows))
    side = jnp.pad(small_all, (0, feat_rows * extra - small_all.shape[0])).reshape(feat_rows, extra)
    qkv_side = lax.all_gather(
        jnp.concatenate([w_qkv, side], axis=1), "dev", axis=0, tiled=True
    )
    full_out = lax.all_gather(w_out, "dev", axis=0, tiled=True)
    full_fc = lax.all_gather(w_fc, "dev", axis=0, tiled=True)
    full_proj = lax.all_gather(w_proj, "dev", axis=0, tiled=True)
    full_qkv = qkv_side[:, : 3 * width]
    side_all = qkv_side[:, 3 * width :].reshape(size, feat_rows * extra).astype(wide)
    vectors = []
    place = 0
    for small in smalls:
        vectors.append(side_all[:, place : place + small.shape[0]].reshape(-1))
        place += small.shape[0]
    gain_one, bias_one, bias_qv, bias_out, gain_two, bias_two, bias_fc, bias_proj = vectors

    firsts = image_firsts(padding, image_ident)
    ext_tokens = jnp.concatenate(
        [shifted(tokens[rows - RIM :], 1), tokens, shifted(tokens[:RIM], -1)], axis=0
    )
    unit_one, scale_one = normed_parts(ext_tokens.astype(wide))
    normed_one = (unit_one * gain_one + bias_one).astype(low)
    normed_own = normed_one[RIM : RIM + rows]
    queries = (
        (dot_nn(normed_own, full_qkv[:, :width]) + bias_qv[:width]).astype(low)
        * HEAD_DIM**-0.5
    ).astype(low)
    kv_bias = jnp.concatenate([jnp.zeros((width,), wide), bias_qv[width:]])
    key_vals = (dot_nn(normed_one, full_qkv[:, width:]) + kv_bias).astype(low)
    attended, lse = attend(firsts, queries, key_vals)

    middle = tokens.astype(wide) + (dot_nn(attended, full_out) + bias_out)
    unit_two, scale_two = normed_parts(middle)
    normed_two = (unit_two * gain_two + bias_two).astype(low)
    hidden = dot_nt(normed_two, full_fc) + bias_fc
    gelu_out, gelu_pull = jax.vjp(quick_gelu, hidden)
    gelu_low = gelu_out.astype(low)
    keep = padding.astype(wide)[:, None]
    output = (keep * (middle + dot_nn(gelu_low, full_proj) + bias_proj)).astype(low)

    grad_result = keep * cotangent.astype(wide)
    grad_result_low = grad_result.astype(low)
    grad_hidden = gelu_pull(dot_nt(grad_result_low, full_proj))[0].astype(low)
    mlp_grads = lax.psum_scatter(
        jnp.concatenate([dot_tn(grad_hidden, normed_two), dot_tn(gelu_low, grad_result_low)], axis=1),
        "dev",
        scatter_dimension=0,
        tiled=True,
    )
    grad_norm_two = dot_nn(grad_hidden, full_fc)
    grad_middle = grad_result + norm_back(unit_two, scale_two, gain_two, grad_norm_two)
    grad_branch = grad_middle.astype(low)
    grad_attended = dot_nt(grad_branch, full_out).astype(low)
    grad_q, grad_k, grad_v = attend_back(firsts, queries, key_vals, grad_attended, lse)

    grad_ext = dot_nt(grad_k, full_qkv[:, width : 2 * width]) + dot_nt(
        grad_v, full_qkv[:, 2 * width :]
    )
    grad_own = grad_ext[RIM : RIM + rows] + dot_nt(grad_q, full_qkv[:, :width])
    head = shifted(grad_ext[rows + RIM :].astype(low), 1).astype(wide)
    tail = shifted(grad_ext[:RIM].astype(low), -1).astype(wide)
    grad_norm_one = grad_own.at[:RIM].add(head).at[rows - RIM :].add(tail)
    unit_own = unit_one[RIM : RIM + rows]
    scale_own = scale_one[RIM : RIM + rows]
    grad_tokens = (grad_middle + norm_back(unit_own, scale_own, gain_one, grad_norm_one)).astype(low)

    def total(values):
        return jnp.sum(values.astype(wide), axis=0)

    small_grads = (
        total(grad_norm_one * unit_own),
        total(grad_norm_one),
        jnp.concatenate([total(grad_q), total(grad_v)]),
        total(grad_branch),
        total(grad_norm_two * unit_two),
        total(grad_norm_two),
        total(grad_hidden),
        total(grad_result),
    )
    small_rows = jnp.concatenate([g.reshape(size, -1) for g in small_grads], axis=1)
    side_grads = jnp.pad(
        small_rows, ((0, 0), (0, feat_rows * extra - small_rows.shape[1]))
    ).reshape(size * feat_rows, extra)
    attn_grads = lax.psum_scatter(
        jnp.concatenate(
            [
                dot_tn(normed_own, grad_q),
                dot_tn(normed_one, grad_k),
                dot_tn(normed_one, grad_v),
                dot_tn(attended, grad_branch),
                side_grads,
            ],
            axis=1,
        ),
        "dev",
        scatter_dimension=0,
        tiled=True,
    )
    side_own = attn_grads[:, 4 * width :].reshape(-1)
    outs = []
    place = 0
    for small in smalls:
        outs.append(side_own[place : place + small.shape[0]])
        place += small.shape[0]
    return (
        output,
        grad_tokens,
        outs[0],
        outs[1],
        attn_grads[:, : 3 * width],
        outs[2],
        attn_grads[:, 3 * width : 4 * width],
        outs[3],
        outs[4],
        outs[5],
        mlp_grads[:, :width],
        outs[6],
        mlp_grads[:, width:],
        outs[7],
    )


def solution(mesh):
    row = P("dev", None)
    line = P("dev")
    return jax.shard_map(
        shards,
        mesh=mesh,
        in_specs=(row, row, line, line, line, line, row, line, row, line, line, line, row, line, row, line),
        out_specs=(row, row, line, line, row, line, row, line, line, line, row, line, row, line),
        check_vma=False,
    )
```

time: 1740 us -> 1120 us (0.64)
  matrix products: 566 us -> 192 us
  waiting for transfers between devices: 402 us -> 623 us
  other arithmetic: 276 us -> 64.3 us
  blocking collectives: 194 us -> 0 us
  local copies, waits for them, and re-layouts: 219 us -> 107 us
  Pallas kernels: 0 us -> 98 us
  loops' own time: 44 us -> 0 us
    dot_general x68 -> x17, matrix products: 566 us -> 192 us  [the longest x6 67 us: dot_nt(): lax.dot_general(a, b, (((1,), (1,)), ((), ())), preferred_element_type=jn...]
    all_gather x4, waiting for transfers between devices: 20.5 us -> 158 us  [the longest x1 61.4 us: shards(): full_proj = lax.all_gather(w_proj, 'dev', axis=0, tiled=True)]
    unnamed x2 -> x0, blocking collectives: 116 us -> none
    pallas_call x0 -> x2, Pallas kernels: none -> 98 us  [the longest x1 51.6 us: attend_back(): pl.pallas_call(attend_back_body, grid_spec=pltpu.PrefetchScalarGridSpec(n...]
    convert_element_type x12 -> x3, other arithmetic: 98.8 us -> 7.52 us  [the longest x1 6.53 us: shards(): (grad_middle + norm_back(unit_own, scale_own, gain_one, grad_norm_one)).a...]
    reduce_scatter x2, waiting for transfers between devices: 380 us -> 463 us  [the longest x1 350 us: shards(): lax.psum_scatter(jnp.concatenate([dot_tn(grad_hidden, normed_two), dot_tn...]
    all_gather x1 -> x0, blocking collectives: 77.9 us -> none  [shards(): lax.all_gather(b_fc, 'dev', axis=0, tiled=True)]
    dynamic_update_slice x14 -> x0, local copies, waits for them, and re-layouts: 62.7 us -> none  [the longest x4 40.8 us: revisit(): lax.dynamic_update_slice_in_dim(value_sums, lax.dynamic_slice_in_dim(valu...]
  transfers between devices with their start and end apart: 10 -> 10, of which waited for: 3 -> 5; matrix products, arithmetic and copies ran while one was open for 24% -> 20% of each run, Pallas kernels for 0% -> 4%
where the time goes in v1:
time: 1120 us; the launch traced here: 1110 us
  waiting for transfers between devices  623 us (56%)
  matrix products  192 us (17%)
  local copies, waits for them, and re-layouts  107 us (10%)
  Pallas kernels  98 us (9%)
  other arithmetic  64.3 us (6%)
  between operations  14.9 us (1%)
    reduce_scatter x1, waiting for transfers between devices, shards(): lax.psum_scatter(jnp.concatenate([dot_tn(grad_hidden, normed_two), dot_tn...  350 us
    reduce_scatter x1, waiting for transfers between devices, shards(): lax.psum_scatter(jnp.concatenate([dot_tn(normed_own, grad_q), dot_tn(norm...  113 us
    dot_general x6, matrix products, dot_nt(): lax.dot_general(a, b, (((1,), (1,)), ((), ())), preferred_element_type=jn...  67 us
    dot_general x6, matrix products, dot_tn(): lax.dot_general(a, b, (((0,), (0,)), ((), ())), preferred_element_type=jn...  66.5 us
    all_gather x1, waiting for transfers between devices, shards(): full_proj = lax.all_gather(w_proj, 'dev', axis=0, tiled=True)  61.4 us
    dot_general x5, matrix products, dot_nn(): lax.dot_general(a, b, (((1,), (0,)), ((), ())), preferred_element_type=jn...  58.8 us
    all_gather x1, waiting for transfers between devices, shards(): full_fc = lax.all_gather(w_fc, 'dev', axis=0, tiled=True)  52 us
    pallas_call x1, Pallas kernels, attend_back(): pl.pallas_call(attend_back_body, grid_spec=pltpu.PrefetchScalarGridSpec(n...  51.6 us
  transfers between devices with their start and end apart: 10, of which 5 were waited for; matrix products, arithmetic and copies ran while one was open for 20% of the time, Pallas kernels for 4%

profile of v1, /device:TPU:0, one launch (start us, length us, event | category | flops | bytes accessed | tf_op | source)
XLA Modules:
  0.0 1107.7 jit_solution(1262156794014615953)
XLA Ops:
  35.1 8.8 concatenate.41
  48.9 44.5 %all-gather.5.cloned.1.call-done = bf16[1024,3200]{1,0:T(8,128)(2,1)} async-done(((bf16[32,3200]{1,0:T(8,128)(2,1)}), bf16[1024,3200]{1,0:T(8,128)(2,1)}) %all-gather.5.cloned.1.call-update) | async-done | bytes 6553616 | tf_op jit(solution)/shard_map/all_gather | solution.py:293
  109.0 14.2 %add_convert_fusion.k_ref.v_ref = bf16[2176,2048]{1,0:T(8,128)(2,1)} fusion(bf16[2176,1024]{0,1:T(8,128)(2,1)S(1)} %get-tuple-element.121, f32[2048]{0:T(1024)S(1)} %concatenate.44, bf16[1024,3200]{1,0:T(8,128)(2,1)} %all-gather.5.cloned.1.call-done), kind=kOutput, calls=%fused_computation.2 | convolution fusion | flops 9135718400 | bytes 17571840 | tf_op jit(solution)/shard_map/dot_general | solution.py:27
  123.2 46.4 %attend.1 = (bf16[1024,1024]{1,0:T(8,128)(2,1)}, f32[4,4,1024]{2,1,0:T(4,128)}) custom-call(s32[16]{0:T(128)} %compare_select_fusion.1.first_ref, bf16[1024,1024]{1,0:T(8,128)(2,1)} %fusion.10.q_ref, bf16[2176,2048]{1,0:T(8,128)(2,1)} %add_convert_fusion.k_ref.v_ref, bf16[2176,2048]{1,0:T(8,128)(2,1)} %add_convert_fusion.k_ref.v_ref), custom_call_target="tpu_custom_call" | custom-call | flops 3103784960 | bytes 16777216 | tf_op jit(solution)/shard_map/attend/pallas_call | solution.py:166
  177.9 52.0 %all-gather.9.cloned.1.call-done = bf16[4096,1024]{1,0:T(8,128)(2,1)} async-done(((bf16[128,1024]{1,0:T(8,128)(2,1)}), bf16[4096,1024]{1,0:T(8,128)(2,1)}) %all-gather.9.cloned.1.call-update) | async-done | bytes 8388624 | tf_op jit(solution)/shard_map/all_gather | solution.py:297
  229.9 17.0 %fusion.25 = f32[1024,4096]{1,0:T(8,128)} fusion(bf16[4096,1024]{1,0:T(8,128)(2,1)} %all-gather.9.cloned.1.call-done, f32[1024,1024]{0,1:T(8,128)} %copy-done.1, f32[1024]{0:T(1024)S(1)} %add.162, f32[1024]{0:T(1024)S(1)} %mul.159, f32[1024]{0:T(1024)S(1)} %add_rsqrt_fusion.1, f32[1024]{0:T(1024)S(1)} %broadcast_multiply_fusion.5), kind=kOutput, calls=%fused_computation.84 | convolution fusion | flops 8595177472 | bytes 29376512 | tf_op jit(solution)/shard_map/dot_general | solution.py:19
  246.9 61.4 %all-gather.11.cloned.1.call-done = bf16[4096,1024]{1,0:T(8,128)(2,1)} async-done(((bf16[128,1024]{1,0:T(8,128)(2,1)}), bf16[4096,1024]{1,0:T(8,128)(2,1)}) %all-gather.11.cloned.1.call-update) | async-done | bytes 8388624 | tf_op jit(solution)/shard_map/all_gather | solution.py:298
  308.3 21.7 %convert_reduce_fusion = (f32[4096]{0:T(1024)S(1)}, bf16[1024,4096]{1,0:T(8,128)(2,1)}) fusion(f32[1024,4096]{1,0:T(8,128)} %fusion.25, f32[4096]{0:T(1024)S(1)} %slice_bitcast_fusion.1, bf16[4096,1024]{1,0:T(8,128)(2,1)} %all-gather.11.cloned.1.call-done, bf16[1024,1024]{0,1:T(8,128)(2,1)S(1)} %copy.94, f32[1024]{0:T(1024)S(1)} %convert_element_type.75), kind=kOutput, calls=%fused_computation.7 | convolution fusion | flops 8655990784 | bytes 35688448 | tf_op jit(solution)/shard_map/dot_general | solution.py:19
  330.1 15.0 %fusion.35 = (f32[1024]{0:T(1024)S(1)}, f32[1024,1024]{1,0:T(8,128)}) fusion(bf16[1024,4096]{1,0:T(8,128)(2,1)} %get-tuple-element.116, bf16[4096,1024]{1,0:T(8,128)(2,1)} %all-gather.9.cloned.1.call-done), kind=kOutput, calls=%fused_computation.93 | convolution fusion | flops 8590982144 | bytes 20975616 | tf_op jit(solution)/shard_map/dot_general | solution.py:27
  362.8 51.6 %attend_back.1 = (bf16[1024,1024]{1,0:T(8,128)(2,1)}, bf16[2176,1024]{1,0:T(8,128)(2,1)}, bf16[2176,1024]{1,0:T(8,128)(2,1)}) custom-call(s32[16]{0:T(128)} %compare_select_fusion.1.first_ref, bf16[1024,1024]{1,0:T(8,128)(2,1)} %fusion.10.q_ref, bf16[2176,2048]{1,0:T(8,128)(2,1)} %add_convert_fusion.k_ref.v_ref, ...), custom_call_target="tpu_custom_call" | custom-call | flops 7759462400 | bytes 16777216 | tf_op jit(solution)/shard_map/attend_back/pallas_call | solution.py:196
  423.5 7.4 fusion.12
  430.9 9.8 fusion.34
  447.2 9.8 convolution_dynamic-update-slice_fusion.2
  456.9 8.9 convolution_dynamic-update-slice_fusion.1
  473.6 7.4 slice_add_fusion
  484.7 12.5 %scatter-add.6 = f32[1024,1024]{0,1:T(8,128)} dynamic-update-slice(f32[1024,1024]{0,1:T(8,128)} %slice_add_fusion, f32[576,1024]{0,1:T(8,128)S(1)} %slice_add_fusion.2, s32[]{:T(128)} %constant.102.clone.1, s32[]{:T(128)} %constant.102.clone.1) | dynamic-update-slice | bytes 4718596 | tf_op jit(solution)/shard_map/scatter-add | solution.py:353
  502.5 13.3 %scatter-add.9 = f32[1024,1024]{0,1:T(8,128)} dynamic-update-slice(f32[1024,1024]{0,1:T(8,128)} %scatter-add.6, f32[576,1024]{0,1:T(8,128)S(1)} %slice_add_fusion.1, s32[]{:T(128)} %constant.103.clone.1, s32[]{:T(128)} %constant.102.clone.1) | dynamic-update-slice | bytes 4718596 | tf_op jit(solution)/shard_map/scatter-add | solution.py:353
  522.1 18.2 %copy.116 = f32[1024,4224]{1,0:T(8,128)} copy(f32[1024,4224]{0,1:T(8,128)} %constant_dynamic-update-slice_fusion) | data formatting | bytes 34603008
  541.0 16.9 %fusion.24 = f32[4096,1024]{0,1:T(8,128)} fusion(bf16[1024,4096]{1,0:T(8,128)(2,1)} %get-tuple-element.116, f32[1024,1024]{0,1:T(8,128)} %copy-done.1, f32[1024]{0:T(1024)S(1)} %copy-done.21, f32[1024]{0:T(1024)S(1)} %mul.159, f32[1024]{0:T(1024)S(1)} %add_rsqrt_fusion.1, f32[1024]{0:T(1024)S(1)} %broadcast_multiply_fusion.5), kind=kOutput, calls=%fused_computation.83 | convolution fusion | flops 8595177472 | bytes 29376512 | tf_op jit(solution)/shard_map/dot_general | solution.py:23
  557.9 16.8 %fusion.18 = f32[4096,1024]{0,1:T(8,128)} fusion(bf16[1024,1024]{0,1:T(8,128)(2,1)S(1)} %copy-done.7, f32[1024]{0:T(1024)S(1)} %convert_element_type.75, f32[1024,4096]{1,0:T(8,128)} %fusion.25, f32[4096]{0:T(1024)S(1)} %copy-done.17), kind=kOutput, calls=%fused_computation.54 | convolution fusion | flops 8622440448 | bytes 35672064 | tf_op jit(solution)/shard_map/dot_general | solution.py:23
  574.7 24.3 %pad_maximum_fusion = f32[4096,2048]{0,1:T(8,128)} fusion(f32[4096,1024]{0,1:T(8,128)} %fusion.18, f32[4096,1024]{0,1:T(8,128)} %fusion.24), kind=kLoop, calls=%fused_computation | loop fusion | flops 8388608 | bytes 67108864 | tf_op jit(solution)/shard_map/concatenate | solution.py:336
  599.9 16.7 %multiply_convert_fusion.1 = bf16[1024,1024]{0,1:T(8,128)(2,1)S(1)} fusion(f32[1024,1024]{0,1:T(8,128)} %copy-done.1, f32[1024]{0:T(1024)S(1)} %add.170, f32[1024]{0:T(1024)S(1)} %convert_element_type.75, bf16[4096,1024]{1,0:T(8,128)(2,1)} %all-gather.11.cloned.1.call-done, f32[1024,4096]{1,0:T(8,128)} %fusion.25, f32[4096]{0:T(1024)S(1)} %copy-done.17), kind=kOutput, calls=%fused_computation.31 | convolution fusion | flops 8623489024 | bytes 31481856 | tf_op jit(solution)/shard_map/dot_general | solution.py:27
  628.3 113.4 %reduce-scatter.7.cloned.1.call-done = f32[32,4224]{1,0:T(8,128)} async-done(((f32[1024,4224]{1,0:T(8,128)}), f32[32,4224]{1,0:T(8,128)}) %reduce-scatter.7.cloned.1.call-update) | async-done | bytes 540688 | tf_op jit(solution)/shard_map/reduce_scatter | solution.py:375
  747.5 349.7 %reduce-scatter.5.cloned.1.call-done = f32[128,2048]{0,1:T(8,128)} async-done(((f32[4096,2048]{0,1:T(8,128)}), f32[128,2048]{0,1:T(8,128)}) %reduce-scatter.5.cloned.1.call-update) | async-done | bytes 1048592 | tf_op jit(solution)/shard_map/reduce_scatter | solution.py:335
  (165 shorter events, 135.2 us)
Async XLA Ops:
  7.2 17.1 %copy-start.5 = (bf16[1024,1024]{1,0:T(8,128)(2,1)S(1)}, bf16[1024,1024]{1,0:T(8,128)(2,1)}, u32[]{:S(2)}) copy-start(bf16[1024,1024]{1,0:T(8,128)(2,1)} %param.20) | copy-start | bytes 6291460
  7.2 86.2 %all-gather.5.cloned.1.call-start = ((), (), s32[]{:S(2)}) async-start(), calls=%async_computation.2 | async-start | bytes 6758400 | tf_op jit(solution)/shard_map/all_gather | solution.py:293
  14.5 155.2 %all-gather.7.cloned.1.call-start = ((), (), s32[]{:S(2)}) async-start(), calls=%async_computation.3 | async-start | bytes 2162688 | tf_op jit(solution)/shard_map/all_gather | solution.py:296
  15.2 214.7 %all-gather.9.cloned.1.call-start = ((), (), s32[]{:S(2)}) async-start(), calls=%async_computation.4 | async-start | bytes 8650752 | tf_op jit(solution)/shard_map/all_gather | solution.py:297
  16.0 292.4 %all-gather.11.cloned.1.call-start = ((), (), s32[]{:S(2)}) async-start(), calls=%async_computation.5 | async-start | bytes 8650752 | tf_op jit(solution)/shard_map/all_gather | solution.py:298
  16.5 10.4 copy-start.18
  16.5 725.1 %reduce-scatter.7.cloned.1.call-start = ((), (), s32[]{:S(2)}) async-start(), calls=%async_computation.7 | async-start | bytes 17842176 | tf_op jit(solution)/shard_map/reduce_scatter | solution.py:375
  19.4 11.6 %collective-permute-start = (bf16[576,1024]{1,0:T(8,128)(2,1)S(1)}, bf16[576,1024]{1,0:T(8,128)(2,1)}, u32[]{:S(2)}, u32[]{:S(2)}) collective-permute-start(bf16[576,1024]{1,0:T(8,128)(2,1)S(1)} %get-tuple-element.126), channel_id=1, source_target_pairs={{0,1},{1,2},{2,3},{3,4},{4,5},{5,6},{6,7},{7,8},{8,9},{9,10},{10,1... | collective-permute-start | bytes 3538952 | tf_op jit(solution)/shard_map/ppermute | solution.py:262
  22.9 9.9 collective-permute-start.1
  29.8 325.3 %copy-start.6 = (bf16[1024,1024]{0,1:T(8,128)(2,1)}, bf16[1024,1024]{0,1:T(8,128)(2,1)S(1)}, u32[]{:S(2)}) copy-start(bf16[1024,1024]{0,1:T(8,128)(2,1)S(1)} %copy.94) | copy-start | bytes 6291460
  48.9 52.9 %copy-start.12 = (f32[2176]{0:T(1024)}, f32[2176]{0:T(1024)S(1)}, u32[]{:S(2)}) copy-start(f32[2176]{0:T(1024)S(1)} %add_rsqrt_fusion) | copy-start | bytes 26116
  95.7 134.2 %copy-start.20 = (f32[1024]{0:T(1024)}, f32[1024]{0:T(1024)S(1)}, u32[]{:S(2)}) copy-start(f32[1024]{0:T(1024)S(1)} %add.162) | copy-start | bytes 12292
  177.9 130.4 %copy-start.16 = (f32[4096]{0:T(1024)}, f32[4096]{0:T(1024)S(1)}, u32[]{:S(2)}) copy-start(f32[4096]{0:T(1024)S(1)} %slice_bitcast_fusion.1) | copy-start | bytes 49156
  414.4 8.0 slice-start.2
  414.4 8.0 slice-start.3
  442.8 38.1 %collective-permute-start.2 = (bf16[576,1024]{1,0:T(8,128)(2,1)}, bf16[576,1024]{1,0:T(8,128)(2,1)S(1)}, u32[]{:S(2)}, u32[]{:S(2)}) collective-permute-start(bf16[576,1024]{1,0:T(8,128)(2,1)} %copy.99), channel_id=1, source_target_pairs={{0,1},{1,2},{2,3},{3,4},{4,5},{5,6},{6,7},{7,8},{8,9},{9,10},{10,1... | collective-permute-start | bytes 3538952 | tf_op jit(solution)/shard_map/ppermute | solution.py:262
  444.2 12.8 %slice-start = ((s8[4456448]{0:T(1024)(128)(4,1)}), s8[262144]{0:T(1024)(128)(4,1)S(1)}, s32[]{:S(2)}) async-start(s8[4456448]{0:T(1024)(128)(4,1)} %bitcast.31), calls=%async_computation.8 | async-start | bytes 524288
  445.6 11.3 %slice-start.1 = ((s8[4456448]{0:T(1024)(128)(4,1)}), s8[4194304]{0:T(1024)(128)(4,1)S(1)}, s32[]{:S(2)}) async-start(s8[4456448]{0:T(1024)(128)(4,1)} %bitcast.31), calls=%async_computation.9 | async-start | bytes 8388608
  445.6 51.6 %collective-permute-start.3 = (bf16[576,1024]{1,0:T(8,128)(2,1)}, bf16[576,1024]{1,0:T(8,128)(2,1)}, u32[]{:S(2)}, u32[]{:S(2)}) collective-permute-start(bf16[576,1024]{1,0:T(8,128)(2,1)} %copy.101), channel_id=1, source_target_pairs={{1,0},{2,1},{3,2},{4,3},{5,4},{6,5},{7,6},{8,7},{9,8},{10,9},{11,1... | collective-permute-start | bytes 3538952 | tf_op jit(solution)/shard_map/ppermute | solution.py:262
  466.3 7.3 copy-start.11
  502.5 13.3 %copy-start.14 = (f32[1024]{0:T(1024)S(1)}, f32[1024]{0:T(1024)}, u32[]{:S(2)}) copy-start(f32[1024]{0:T(1024)} %copy-done.13) | copy-start | bytes 12292
  540.3 17.6 %copy-start.7 = (bf16[1024,1024]{0,1:T(8,128)(2,1)S(1)}, bf16[1024,1024]{0,1:T(8,128)(2,1)}, u32[]{:S(2)}) copy-start(bf16[1024,1024]{0,1:T(8,128)(2,1)} %copy-done.6) | copy-start | bytes 6291460
  540.4 17.5 %copy-start.17 = (f32[4096]{0:T(1024)S(1)}, f32[4096]{0:T(1024)}, u32[]{:S(2)}) copy-start(f32[4096]{0:T(1024)} %copy-done.16) | copy-start | bytes 49156
  540.4 556.7 %reduce-scatter.5.cloned.1.call-start = ((), (), s32[]{:S(2)}) async-start(), calls=%async_computation.6 | async-start | bytes 34603008 | tf_op jit(solution)/shard_map/reduce_scatter | solution.py:335
  (14 other events, 61.1 us)
Sparse Core Ops, SparseCore 0:
  14.6 78.7 all-gather.4
  96.3 54.7 all-gather.6
  154.0 75.8 all-gather.8
  232.6 75.6 all-gather.10
  540.5 201.1 reduce-scatter.6
  743.8 353.2 reduce-scatter.4

commit v2 on v1

--- a/solution.py
+++ b/solution.py
@@ -1,5 +1,6 @@
 import jax
 import jax.numpy as jnp
+import numpy as np
 from jax import lax
 from jax.experimental import pallas as pl
 from jax.experimental.pallas import tpu as pltpu
@@ -99,7 +100,7 @@
 
 
 def attend_back_body(
-    first_ref, q_ref, k_ref, v_ref, grad_ref, lse_ref, dq_ref, dk_ref, dv_ref, dk_sum, dv_sum
+    first_ref, q_ref, k_ref, v_ref, grad_ref, lse_ref, dq_ref, dkv_ref, dk_sum, dv_sum
 ):
     rows = q_ref.shape[0]
     tiles = rows // TILE
@@ -147,13 +148,13 @@
         return carry
 
     lax.fori_loop(0, tiles, tile, 0)
-    dk_ref[...] = dk_sum[...].astype(jnp.bfloat16)
-    dv_ref[...] = dv_sum[...].astype(jnp.bfloat16)
+    dkv_ref[:, :LANES] = dk_sum[...].astype(jnp.bfloat16)
+    dkv_ref[:, LANES:] = dv_sum[...].astype(jnp.bfloat16)
 
 
 def attention_cost(rows, width, products):
     return pl.CostEstimate(
-        flops=2 * products * 10 * TILE * KEYS * width,
+        flops=2 * products * 10 * TILE * KEYS * width * 8,
         bytes_accessed=16 * rows * width,
         transcendentals=10 * TILE * KEYS * (width // HEAD_DIM),
     )
@@ -170,8 +171,8 @@
             grid=(groups,),
             in_specs=[
                 pl.BlockSpec((rows, LANES), lambda g, f: (0, g)),
-                pl.BlockSpec((ext, LANES), lambda g, f: (0, g)),
-                pl.BlockSpec((ext, LANES), lambda g, f: (0, g + groups)),
+                pl.BlockSpec((ext, LANES), lambda g, f: (0, 2 * g)),
+                pl.BlockSpec((ext, LANES), lambda g, f: (0, 2 * g + 1)),
             ],
             out_specs=[
                 pl.BlockSpec((rows, LANES), lambda g, f: (0, g)),
@@ -187,12 +188,12 @@
     )(firsts, queries, key_vals, key_vals)
 
 
-def attend_back(firsts, queries, key_vals, grads, lse):
+def attend_back(firsts, queries, key_vals, grads, lse, part):
     rows, width = queries.shape
     ext = key_vals.shape[0]
-    groups = width // LANES
-    own = pl.BlockSpec((rows, LANES), lambda g, f: (0, g))
-    wide = pl.BlockSpec((ext, LANES), lambda g, f: (0, g))
+    groups = width // LANES // 2
+    base = part * groups
+    own = pl.BlockSpec((rows, LANES), lambda g, f: (0, base + g))
     return pl.pallas_call(
         attend_back_body,
         grid_spec=pltpu.PrefetchScalarGridSpec(
@@ -200,22 +201,31 @@
             grid=(groups,),
             in_specs=[
                 own,
-                wide,
-                pl.BlockSpec((ext, LANES), lambda g, f: (0, g + groups)),
+                pl.BlockSpec((ext, LANES), lambda g, f: (0, 2 * (base + g))),
+                pl.BlockSpec((ext, LANES), lambda g, f: (0, 2 * (base + g) + 1)),
                 own,
-                pl.BlockSpec((1, LANES // HEAD_DIM, rows), lambda g, f: (g, 0, 0)),
+                pl.BlockSpec((1, LANES // HEAD_DIM, rows), lambda g, f: (base + g, 0, 0)),
             ],
-            out_specs=[own, wide, wide],
+            out_specs=[
+                pl.BlockSpec((rows, LANES), lambda g, f: (0, g)),
+                pl.BlockSpec((ext, 2 * LANES), lambda g, f: (0, g)),
+            ],
             scratch_shapes=[pltpu.VMEM((ext, LANES), jnp.float32)] * 2,
         ),
         out_shape=[
-            jax.ShapeDtypeStruct((rows, width), jnp.bfloat16),
-            jax.ShapeDtypeStruct((ext, width), jnp.bfloat16),
+            jax.ShapeDtypeStruct((rows, width // 2), jnp.bfloat16),
             jax.ShapeDtypeStruct((ext, width), jnp.bfloat16),
         ],
-        cost_estimate=attention_cost(rows, width, 5),
+        cost_estimate=attention_cost(rows, width // 2, 5),
         name="attend_back",
     )(firsts, queries, key_vals, key_vals, grads, lse)
+
+
+def by_group(keys, values):
+    parts = []
+    for at in range(0, keys.shape[-1], LANES):
+        parts += [keys[..., at : at + LANES], values[..., at : at + LANES]]
+    return parts
 
 
 def image_firsts(padding, ident):
@@ -260,6 +270,76 @@
     size = lax.axis_size("dev")
     pairs = [(i, i + by) for i in range(size) if 0 <= i + by < size]
     return lax.ppermute(value, "dev", pairs)
+
+
+class Rings:
+    def __init__(self, size):
+        bits = size.bit_length() - 1
+        self.size = size
+        self.top = bits - 2
+        middle = list(range(1, self.top))
+        self.orders = (middle, middle[::-1])
+        self.stages = len(middle)
+        halves = []
+        for order in self.orders:
+            blocks = [(0, r) for r in range(4)]
+            for bit in order:
+                blocks = blocks + [(mask ^ (1 << bit), r) for mask, r in blocks]
+            halves.append(blocks)
+        self.blocks = [
+            halves[core] + [(mask ^ 1, r) for mask, r in halves[1 - core]] for core in range(2)
+        ]
+
+    def rotated(self, device, by):
+        low = device % (1 << self.top)
+        return (((device >> self.top) + by) % 4 << self.top) | low
+
+    def permute(self, value, target):
+        return lax.ppermute(value, "dev", [(i, target(i)) for i in range(self.size)])
+
+    def turn(self, value, by):
+        return self.permute(value, lambda i: self.rotated(i, by))
+
+    def pair(self, value, stage):
+        return self.permute(value, lambda i: i ^ (1 << self.orders[i & 1][stage]))
+
+    def swap(self, value):
+        return self.permute(value, lambda i: i ^ 1)
+
+    def owners(self):
+        me = lax.axis_index("dev")
+        lists = []
+        for core in range(2):
+            masks = np.array([mask for mask, _ in self.blocks[core]], np.int32)
+            turns = np.array([r for _, r in self.blocks[core]], np.int32)
+            low = (me ^ masks) & ((1 << self.top) - 1)
+            lists.append((((me >> self.top) + turns) & 3) << self.top | low)
+        return jnp.where(me & 1 == 0, lists[0], lists[1])
+
+    def quad(self, block):
+        return jnp.concatenate([block] + [self.turn(block, -r) for r in (1, 2, 3)], axis=0)
+
+    def cut(self, total):
+        at = total.shape[0] // 2
+        return total[:at], total[at:].astype(jnp.bfloat16)
+
+    def quarters(self, total):
+        rows = total.shape[0] // 4
+        sent = [total[r * rows : (r + 1) * rows].astype(jnp.bfloat16) for r in (1, 2, 3)]
+        return total[:rows], sent
+
+    def turned(self, parts):
+        return [self.turn(part, r) for r, part in zip((1, 2, 3), parts)]
+
+
+def added(kept, *received):
+    for part in received:
+        kept = kept + part.astype(jnp.float32)
+    return kept
+
+
+def after(value, *others):
+    return lax.optimization_barrier((value, others))[0]
 
 
 def shards(
@@ -287,22 +367,36 @@
     rows = tokens.shape[0]
     feat_rows = w_qkv.shape[0]
     smalls = (ln1_gain, ln1_bias, b_qv, b_out, ln2_gain, ln2_bias, b_fc, b_proj)
-    small_all = jnp.concatenate(smalls)
-    extra = 128 * -(-small_all.shape[0] // (128 * feat_rows))
-    side = jnp.pad(small_all, (0, feat_rows * extra - small_all.shape[0])).reshape(feat_rows, extra)
+    extra = 128
+    rings = Rings(size)
+    owners = rings.owners()
+    side = jnp.concatenate(smalls)
+    side = jnp.pad(side, (0, feat_rows * extra - side.shape[0])).reshape(feat_rows, extra)
     qkv_side = lax.all_gather(
-        jnp.concatenate([w_qkv, side], axis=1), "dev", axis=0, tiled=True
+        jnp.concatenate(
+            [w_qkv[:, :width]]
+            + by_group(w_qkv[:, width : 2 * width], w_qkv[:, 2 * width :])
+            + [side],
+            axis=1,
+        ),
+        "dev", axis=0, tiled=True
     )
     full_out = lax.all_gather(w_out, "dev", axis=0, tiled=True)
-    full_fc = lax.all_gather(w_fc, "dev", axis=0, tiled=True)
-    full_proj = lax.all_gather(w_proj, "dev", axis=0, tiled=True)
+    halves = [rings.quad(w_fc), rings.quad(w_proj)]
+    last = rings.stages - 1
+    for stage in range(last):
+        halves = [jnp.concatenate([h, rings.pair(h, stage)], axis=0) for h in halves]
+    halves = [(h, rings.pair(h, last)) for h in halves]
     full_qkv = qkv_side[:, : 3 * width]
     side_all = qkv_side[:, 3 * width :].reshape(size, feat_rows * extra).astype(wide)
     vectors = []
     place = 0
     for small in smalls:
-        vectors.append(side_all[:, place : place + small.shape[0]].reshape(-1))
+        vectors.append(side_all[:, place : place + small.shape[0]])
         place += small.shape[0]
+    chosen = (owners[:, None] == jnp.arange(size, dtype=jnp.int32)[None, :])[:, :, None]
+    vectors[6] = jnp.sum(jnp.where(chosen, vectors[6][None], 0.0), axis=1)
+    vectors = [v.reshape(-1) for v in vectors]
     gain_one, bias_one, bias_qv, bias_out, gain_two, bias_two, bias_fc, bias_proj = vectors
 
     firsts = image_firsts(padding, image_ident)
@@ -316,98 +410,184 @@
         (dot_nn(normed_own, full_qkv[:, :width]) + bias_qv[:width]).astype(low)
         * HEAD_DIM**-0.5
     ).astype(low)
-    kv_bias = jnp.concatenate([jnp.zeros((width,), wide), bias_qv[width:]])
+    kv_bias = jnp.concatenate(by_group(jnp.zeros((width,), wide), bias_qv[width:]))
     key_vals = (dot_nn(normed_one, full_qkv[:, width:]) + kv_bias).astype(low)
+    feature = jnp.arange(width, dtype=jnp.int32)
+    wanted = (owners[:, None] * feat_rows + jnp.arange(feat_rows, dtype=jnp.int32)).reshape(-1)
+    reorder = (feature[:, None] == wanted[None, :]).astype(low)
+    normed_turned = dot_nn(normed_one, reorder).astype(low)
+    key_vals, halves = lax.optimization_barrier((key_vals, halves))
+    halves = [jnp.concatenate(h, axis=0) for h in halves]
+    queries, halves = lax.optimization_barrier((queries, halves))
+    (fc_own, proj_own), (fc_other, proj_other) = halves, [rings.swap(h) for h in halves]
     attended, lse = attend(firsts, queries, key_vals)
 
     middle = tokens.astype(wide) + (dot_nn(attended, full_out) + bias_out)
     unit_two, scale_two = normed_parts(middle)
     normed_two = (unit_two * gain_two + bias_two).astype(low)
-    hidden = dot_nt(normed_two, full_fc) + bias_fc
-    gelu_out, gelu_pull = jax.vjp(quick_gelu, hidden)
-    gelu_low = gelu_out.astype(low)
     keep = padding.astype(wide)[:, None]
-    output = (keep * (middle + dot_nn(gelu_low, full_proj) + bias_proj)).astype(low)
-
     grad_result = keep * cotangent.astype(wide)
     grad_result_low = grad_result.astype(low)
-    grad_hidden = gelu_pull(dot_nt(grad_result_low, full_proj))[0].astype(low)
-    mlp_grads = lax.psum_scatter(
-        jnp.concatenate([dot_tn(grad_hidden, normed_two), dot_tn(gelu_low, grad_result_low)], axis=1),
-        "dev",
-        scatter_dimension=0,
-        tiled=True,
-    )
-    grad_norm_two = dot_nn(grad_hidden, full_fc)
+    half = fc_own.shape[0]
+
+    def up(fc_part, proj_part, bias_part):
+        hidden, pull = jax.vjp(quick_gelu, dot_nt(normed_two, fc_part) + bias_part)
+        return hidden.astype(low), pull
+
+    def down(pull, proj_part):
+        return pull(dot_nt(grad_result_low, proj_part))[0].astype(low)
+
+    gelu_own, pull_own = up(fc_own, proj_own, bias_fc[:half])
+    gelu_other, pull_other = up(fc_other, proj_other, bias_fc[half:])
+    proj_sent = rings.swap(dot_tn(gelu_other, grad_result_low).astype(low))
+    proj_kept = dot_tn(gelu_own, grad_result_low)
+    grad_hidden_own = down(pull_own, proj_own)
+    grad_hidden_other = down(pull_other, proj_other)
+    fc_sent = rings.swap(dot_tn(grad_hidden_other, normed_two).astype(low))
+    fc_kept = dot_tn(grad_hidden_own, normed_two)
+    proj_kept, proj_cut = rings.cut(added(proj_kept, proj_sent))
+    proj_sent = rings.pair(proj_cut, last)
+    up_own, up_other = dot_nn(gelu_own, proj_own), dot_nn(gelu_other, proj_other)
+    output = (keep * (middle + up_own + up_other + bias_proj)).astype(low)
+    down_own, down_other = dot_nn(grad_hidden_own, fc_own), dot_nn(grad_hidden_other, fc_other)
+    fc_kept, fc_cut = rings.cut(added(fc_kept, fc_sent))
+    grad_norm_two = down_own + down_other
     grad_middle = grad_result + norm_back(unit_two, scale_two, gain_two, grad_norm_two)
     grad_branch = grad_middle.astype(low)
     grad_attended = dot_nt(grad_branch, full_out).astype(low)
-    grad_q, grad_k, grad_v = attend_back(firsts, queries, key_vals, grad_attended, lse)
-
-    grad_ext = dot_nt(grad_k, full_qkv[:, width : 2 * width]) + dot_nt(
-        grad_v, full_qkv[:, 2 * width :]
-    )
-    grad_own = grad_ext[RIM : RIM + rows] + dot_nt(grad_q, full_qkv[:, :width])
+
+    def total(values):
+        return jnp.sum(values.astype(wide), axis=0)
+
+    hidden_sums = jnp.concatenate([total(grad_hidden_own), total(grad_hidden_other)])
+    hidden_sums = jnp.sum(jnp.where(chosen, hidden_sums.reshape(size, 1, -1), 0.0), axis=0)
+    def sided(vectors):
+        lines = jnp.concatenate([g.reshape(size, -1) for g in vectors], axis=1)
+        lines = jnp.pad(lines, ((0, 0), (0, feat_rows * extra - lines.shape[1])))
+        return lines.reshape(width, extra)
+
+    def unsided(flat, vectors):
+        parts = []
+        at = 0
+        for vector in vectors:
+            parts.append(flat[at : at + vector.shape[0]])
+            at += vector.shape[0]
+        return parts
+
+    def scattered(values):
+        return lax.psum_scatter(values, "dev", scatter_dimension=0, tiled=True)
+
+    turned_own = normed_turned[RIM : RIM + rows]
+    near, far = slice(0, width // 2), slice(width // 2, width)
+
+    def products(lines, grad_q, grad_kv):
+        return jnp.concatenate(
+            [dot_tn(turned_own[:, lines], grad_q), dot_tn(normed_turned[:, lines], grad_kv)], axis=1
+        )
+
+    out_product = dot_tn(attended, grad_branch)
+    grad_attended = after(grad_attended, output, fc_cut, proj_cut, out_product)
+    fc_sent = rings.pair(fc_cut, last)
+    grad_out = scattered(out_product)
+    first_q, first_kv = attend_back(firsts, queries, key_vals, grad_attended, lse, 0)
+
+    first_kv, fc_sent, proj_sent = lax.optimization_barrier((first_kv, fc_sent, proj_sent))
+    for stage in reversed(range(last)):
+        fc_kept, fc_cut = rings.cut(added(fc_kept, fc_sent))
+        proj_kept, proj_cut = rings.cut(added(proj_kept, proj_sent))
+        fc_sent, proj_sent = rings.pair(fc_cut, stage), rings.pair(proj_cut, stage)
+    first_cut = products(far, first_q, first_kv).astype(low)
+    first_sent = rings.swap(first_cut)
+    first_kept = products(near, first_q, first_kv)
+    grad_attended = after(grad_attended, first_kept, first_cut, fc_cut, proj_cut)
+    second_q, second_kv = attend_back(firsts, queries, key_vals, grad_attended, lse, 1)
+
+    second_kv, fc_sent, proj_sent, first_sent, grad_out = lax.optimization_barrier(
+        (second_kv, fc_sent, proj_sent, first_sent, grad_out)
+    )
+    fc_kept, fc_cut = rings.quarters(added(fc_kept, fc_sent))
+    proj_kept, proj_cut = rings.quarters(added(proj_kept, proj_sent))
+    first_kept, first_cut = rings.cut(added(first_kept, first_sent))
+    first_sent = rings.pair(first_cut, last)
+    fc_sent, proj_sent = rings.turned(fc_cut), rings.turned(proj_cut)
+    second_kv = after(second_kv, fc_cut, proj_cut, first_cut)
+    second_cut = products(far, second_q, second_kv).astype(low)
+    second_sent = rings.swap(second_cut)
+    second_kept = products(near, second_q, after(second_kv, second_cut))
+    second_sent, first_sent, second_kept = lax.optimization_barrier(
+        (second_sent, first_sent, second_kept)
+    )
+    second_kept, second_cut = rings.cut(added(second_kept, second_sent))
+    second_sent = rings.pair(second_cut, last)
+    for stage in reversed(range(last)):
+        first_kept, first_cut = rings.cut(added(first_kept, first_sent))
+        first_sent = rings.pair(first_cut, stage)
+    w_kv = full_qkv[:, width:]
+    grad_ext = dot_nt(after(first_kv, second_cut, first_cut), w_kv[:, :width])
+    grad_ext, first_sent, second_sent = lax.optimization_barrier((grad_ext, first_sent, second_sent))
+    for stage in reversed(range(last)):
+        second_kept, second_cut = rings.cut(added(second_kept, second_sent))
+        second_sent = rings.pair(second_cut, stage)
+    first_kept, first_cut = rings.quarters(added(first_kept, first_sent))
+    first_sent = rings.turned(first_cut)
+    grad_ext = grad_ext + dot_nt(after(second_kv, second_cut, first_cut), w_kv[:, width:])
+    grad_q = jnp.concatenate([first_q, second_q], axis=1)
+    grad_by_q = dot_nt(grad_q, full_qkv[:, :width])
+    grad_own = grad_ext[RIM : RIM + rows] + grad_by_q
     head = shifted(grad_ext[rows + RIM :].astype(low), 1).astype(wide)
     tail = shifted(grad_ext[:RIM].astype(low), -1).astype(wide)
-    grad_norm_one = grad_own.at[:RIM].add(head).at[rows - RIM :].add(tail)
+    grad_own, second_sent = lax.optimization_barrier((grad_own, second_sent))
+    second_kept, second_cut = rings.quarters(added(second_kept, second_sent))
+    second_sent = rings.turned(second_cut)
+    grad_norm_one = (
+        grad_own
+        + jnp.pad(head, ((0, rows - RIM), (0, 0)))
+        + jnp.pad(tail, ((rows - RIM, 0), (0, 0)))
+    )
     unit_own = unit_one[RIM : RIM + rows]
     scale_own = scale_one[RIM : RIM + rows]
     grad_tokens = (grad_middle + norm_back(unit_own, scale_own, gain_one, grad_norm_one)).astype(low)
 
-    def total(values):
-        return jnp.sum(values.astype(wide), axis=0)
-
-    small_grads = (
-        total(grad_norm_one * unit_own),
-        total(grad_norm_one),
-        jnp.concatenate([total(grad_q), total(grad_v)]),
-        total(grad_branch),
-        total(grad_norm_two * unit_two),
-        total(grad_norm_two),
-        total(grad_hidden),
-        total(grad_result),
-    )
-    small_rows = jnp.concatenate([g.reshape(size, -1) for g in small_grads], axis=1)
-    side_grads = jnp.pad(
-        small_rows, ((0, 0), (0, feat_rows * extra - small_rows.shape[1]))
-    ).reshape(size * feat_rows, extra)
-    attn_grads = lax.psum_scatter(
-        jnp.concatenate(
-            [
-                dot_tn(normed_own, grad_q),
-                dot_tn(normed_one, grad_k),
-                dot_tn(normed_one, grad_v),
-                dot_tn(attended, grad_branch),
-                side_grads,
-            ],
-            axis=1,
-        ),
-        "dev",
-        scatter_dimension=0,
-        tiled=True,
-    )
-    side_own = attn_grads[:, 4 * width :].reshape(-1)
-    outs = []
-    place = 0
-    for small in smalls:
-        outs.append(side_own[place : place + small.shape[0]])
-        place += small.shape[0]
+    grad_fc, grad_proj = added(fc_kept, *fc_sent), added(proj_kept, *proj_sent)
+    grad_first, grad_second = added(first_kept, *first_sent), added(second_kept, *second_sent)
+    value_sums = [total(first_kv).reshape(-1, 2, LANES), total(second_kv).reshape(-1, 2, LANES)]
+    value_sums = jnp.concatenate(value_sums, axis=0)[:, 1].reshape(-1)
+    side_grads = scattered(
+        sided(
+            (
+                total(grad_ext * unit_one) + total(grad_by_q * unit_own),
+                total(grad_ext) + total(grad_by_q),
+                jnp.concatenate([total(grad_q), value_sums]),
+                total(grad_branch),
+                total(grad_norm_two * unit_two),
+                total(grad_norm_two),
+                hidden_sums,
+                total(grad_result),
+            )
+        )
+    )
+    small_outs = unsided(side_grads.reshape(-1), smalls)
+    both = (grad_first, grad_second)
+    columns = [part[:, : width // 2] for part in both]
+    for which in range(2):
+        for part in both:
+            for at in range(width // 2, part.shape[1], 2 * LANES):
+                columns.append(part[:, at + which * LANES : at + which * LANES + LANES])
     return (
         output,
         grad_tokens,
-        outs[0],
-        outs[1],
-        attn_grads[:, : 3 * width],
-        outs[2],
-        attn_grads[:, 3 * width : 4 * width],
-        outs[3],
-        outs[4],
-        outs[5],
-        mlp_grads[:, :width],
-        outs[6],
-        mlp_grads[:, width:],
-        outs[7],
+        small_outs[0],
+        small_outs[1],
+        jnp.concatenate(columns, axis=1),
+        small_outs[2],
+        grad_out,
+        small_outs[3],
+        small_outs[4],
+        small_outs[5],
+        grad_fc,
+        small_outs[6],
+        grad_proj,
+        small_outs[7],
     )
 
 

time: 1120 us -> 888 us (0.79)
  waiting for transfers between devices: 623 us -> 252 us
  starting transfers between devices: 7.97 us -> 82 us
  other arithmetic: 64.3 us -> 97.9 us
  matrix products: 192 us -> 209 us
    reduce_scatter x2, waiting for transfers between devices: 463 us -> 134 us  [scattered(): return lax.psum_scatter(values, 'dev', scatter_dimension=0, tiled=True)]
    all_gather x3 -> x1, waiting for transfers between devices: 158 us -> 0.01 us  [shards(): lax.all_gather(jnp.concatenate([w_qkv[:, :width]] + by_group(w_qkv[:, wid...]
    ppermute x0 -> x36, waiting for transfers between devices: none -> 118 us  [permute(): lax.ppermute(value, 'dev', [(i, target(i)) for i in range(self.size)])]
    ppermute x0 -> x36, starting transfers between devices: none -> 72.5 us  [permute(): lax.ppermute(value, 'dev', [(i, target(i)) for i in range(self.size)])]
    scatter-add x2 -> x0, local copies, waits for them, and re-layouts: 25.8 us -> none  [shards(): grad_norm_one = grad_own.at[:RIM].add(head).at[rows - RIM:].add(tail)]
    add x2 -> x14, other arithmetic: 5.17 us -> 25.3 us  [the longest x10 17.7 us: added(): kept = kept + part.astype(jnp.float32)]
    dot_general x5 -> x8, matrix products: 58.8 us -> 75.9 us  [dot_nn(): lax.dot_general(a, b, (((1,), (0,)), ((), ())), preferred_element_type=jn...]
    concatenate x3 -> x7, other arithmetic: 26 us -> 13.4 us  [the longest x1 6.16 us: shards(): halves = [jnp.concatenate(h, axis=0) for h in halves]]
  transfers between devices with their start and end apart: 10 -> 44, of which waited for: 5 -> 14; matrix products, arithmetic and copies ran while one was open for 20% -> 40% of each run, Pallas kernels for 4% -> 12%
where the time goes in v2:
time: 888 us; the launch traced here: 875 us
  waiting for transfers between devices  252 us (28%)
  matrix products  209 us (24%)
  local copies, waits for them, and re-layouts  117 us (13%)
  Pallas kernels  102 us (11%)
  other arithmetic  97.9 us (11%)
  starting transfers between devices  82 us (9%)
  between operations  15.5 us (2%)
    reduce_scatter x2, waiting for transfers between devices, scattered(): return lax.psum_scatter(values, 'dev', scatter_dimension=0, tiled=True)  134 us
    ppermute x36, waiting for transfers between devices, permute(): lax.ppermute(value, 'dev', [(i, target(i)) for i in range(self.size)])  118 us
    dot_general x8, matrix products, dot_nn(): lax.dot_general(a, b, (((1,), (0,)), ((), ())), preferred_element_type=jn...  75.9 us
    ppermute x36, starting transfers between devices, permute(): lax.ppermute(value, 'dev', [(i, target(i)) for i in range(self.size)])  72.5 us
    dot_general x8, matrix products, dot_nt(): lax.dot_general(a, b, (((1,), (1,)), ((), ())), preferred_element_type=jn...  67.4 us
    dot_general x13, matrix products, dot_tn(): lax.dot_general(a, b, (((0,), (0,)), ((), ())), preferred_element_type=jn...  65.8 us
    pallas_call x2, Pallas kernels, attend_back(): pl.pallas_call(attend_back_body, grid_spec=pltpu.PrefetchScalarGridSpec(n...  55.6 us
    unnamed x197, local copies, waits for them, and re-layouts  47.8 us
  transfers between devices with their start and end apart: 44, of which 14 were waited for; matrix products, arithmetic and copies ran while one was open for 40% of the time, Pallas kernels for 12%

profile of v2, /device:TPU:0, one launch (start us, length us, event | category | flops | bytes accessed | tf_op | source)
XLA Modules:
  0.0 875.2 jit_solution(2811035498708534674)
XLA Ops:
  37.1 16.8 %collective-permute-done.3 = bf16[128,1024]{1,0:T(8,128)(2,1)} collective-permute-done((bf16[128,1024]{1,0:T(8,128)(2,1)}, bf16[128,1024]{1,0:T(8,128)(2,1)}, u32[]{:S(2)}, u32[]{:S(2)}) %collective-permute-start.3) | collective-permute-done | bytes 262176 | tf_op jit(solution)/shard_map/ppermute | solution.py:298
  116.8 16.5 %collective-permute-done.10 = bf16[512,1024]{1,0:T(8,128)(2,1)} collective-permute-done((bf16[512,1024]{1,0:T(8,128)(2,1)}, bf16[512,1024]{1,0:T(8,128)(2,1)}, u32[]{:S(2)}, u32[]{:S(2)}) %collective-permute-start.10) | collective-permute-done | bytes 1048608 | tf_op jit(solution)/shard_map/ppermute | solution.py:298
  141.8 11.6 %add_convert_fusion.k_ref.v_ref = bf16[2176,2048]{1,0:T(8,128)(2,1)} fusion(bf16[2176,1024]{0,1:T(8,128)(2,1)S(1)} %add_convert_fusion.1, f32[2048]{0:T(1024)S(1)} %constant_dynamic-update-slice_fusion.33, bf16[1024,3200]{1,0:T(8,128)(2,1)S(1)} %copy-done.54), kind=kOutput, calls=%fused_computation | convolution fusion | flops 9135718400 | bytes 17571840 | tf_op jit(solution)/shard_map/dot_general | solution.py:28
  153.8 12.7 %collective-permute-done.11 = bf16[1024,1024]{1,0:T(8,128)(2,1)} collective-permute-done((bf16[1024,1024]{1,0:T(8,128)(2,1)}, bf16[1024,1024]{1,0:T(8,128)(2,1)}, u32[]{:S(2)}, u32[]{:S(2)}) %collective-permute-start.11) | collective-permute-done | bytes 2097184 | tf_op jit(solution)/shard_map/ppermute | solution.py:298
  179.4 46.7 %attend.1 = (bf16[1024,1024]{1,0:T(8,128)(2,1)}, f32[4,4,1024]{2,1,0:T(4,128)}) custom-call(s32[16]{0:T(128)} %compare_select_fusion.1.first_ref, bf16[1024,1024]{1,0:T(8,128)(2,1)} %fusion.14.q_ref, bf16[2176,2048]{1,0:T(8,128)(2,1)} %add_convert_fusion.k_ref.v_ref, bf16[2176,2048]{1,0:T(8,128)(2,1)} %add_convert_fusion.k_ref.v_ref), custom_call_target="tpu_custom_call" | custom-call | flops 24830279680 | bytes 16777216 | tf_op jit(solution)/shard_map/attend/pallas_call | solution.py:167
  246.5 9.9 %fusion.91 = f32[1024,1024]{0,1:T(8,128)} fusion(bf16[1024,2048]{1,0:T(8,128)(2,1)S(1)} %get-tuple-element.207, bf16[2048,1024]{1,0:T(8,128)(2,1)} %get-tuple-element.58), kind=kOutput, calls=%fused_computation.215 | convolution fusion | flops 4294967296 | bytes 12582912 | tf_op jit(solution)/shard_map/dot_general | solution.py:28
  256.4 11.5 %convert_reduce_fusion.4 = (f32[2048]{0:T(1024)S(1)}, bf16[1024,2048]{1,0:T(8,128)(2,1)}) fusion(f32[1024,2048]{1,0:T(8,128)S(1)} %get-tuple-element.208, f32[2048]{0:T(1024)S(1)} %get-tuple-element.204, bf16[2048,1024]{1,0:T(8,128)(2,1)} %get-tuple-element.58, bf16[1024,1024]{0,1:T(8,128)(2,1)S(1)} %copy.101, f32[1024]{0:T(1024)S(1)} %copy-done.50), kind=kOutput, calls=%fused_computation.21 | convolution fusion | flops 4329568256 | bytes 18894848 | tf_op jit(solution)/shard_map/dot_general | solution.py:20
  274.6 10.3 %fusion.93 = f32[1024,1024]{0,1:T(8,128)} fusion(bf16[1024,2048]{1,0:T(8,128)(2,1)} %get-tuple-element.215, bf16[2048,1024]{1,0:T(8,128)(2,1)} %get-tuple-element.57), kind=kOutput, calls=%fused_computation.217 | convolution fusion | flops 4294967296 | bytes 12582912 | tf_op jit(solution)/shard_map/dot_general | solution.py:28
  314.6 12.8 %multiply_convert_fusion.2 = bf16[1024,1024]{0,1:T(8,128)(2,1)} fusion(f32[1024,1024]{0,1:T(8,128)S(1)} %copy-done.2, f32[1024,1024]{0,1:T(8,128)} %fusion.91, f32[1024]{0:T(1024)S(1)} %add.305, f32[1024]{0:T(1024)S(1)} %copy-done.50, bf16[2048,1024]{1,0:T(8,128)(2,1)} %collective-permute-done.13, f32[1024,2048]{1,0:T(8,128)} %copy-done.59, ...), kind=kOutput, calls=%fused_computation.50 | convolution fusion | flops 4314890240 | bytes 23085056 | tf_op jit(solution)/shard_map/dot_general | solution.py:28
  327.3 12.6 %multiply_reduce_fusion.1 = (f32[1024]{0:T(1024)S(1)}, f32[1024]{0:T(1024)S(1)}, f32[1024]{0:T(1024)S(1)}, f32[1024]{0:T(1024)S(1)}, f32[1024,1024]{0,1:T(8,128)}) fusion(f32[1024,1024]{0,1:T(8,128)S(1)} %copy-done.2, f32[1024]{0:T(1024)S(1)} %copy-done.46, f32[1024]{0:T(1024)S(1)} %copy-done.42, f32[1024]{0:T(1024)S(1)} %copy-done.44, ...), kind=kOutput, calls=%fused_computation.37 | convolution fusion | flops 4305448960 | bytes 21000192 | tf_op jit(solution)/shard_map/dot_general | solution.py:28
  365.7 9.5 %convert_add_fusion.1 = f32[2048,1024]{1,0:T(8,128)S(1)} fusion(bf16[2048,1024]{1,0:T(8,128)(2,1)} %collective-permute-done.14, bf16[1024,2048]{1,0:T(8,128)(2,1)S(1)} %copy-done.62, bf16[1024,1024]{0,1:T(8,128)(2,1)S(1)} %copy-done.17), kind=kOutput, calls=%fused_computation.23 | convolution fusion | flops 4299161600 | bytes 18874368 | tf_op jit(solution)/shard_map/dot_general | solution.py:24
  380.5 9.7 %convert_add_fusion = f32[2048,1024]{1,0:T(8,128)S(1)} fusion(bf16[2048,1024]{1,0:T(8,128)(2,1)} %collective-permute-done.15, bf16[1024,2048]{1,0:T(8,128)(2,1)S(1)} %copy-done.61, bf16[1024,1024]{0,1:T(8,128)(2,1)S(1)} %copy.101, f32[1024]{0:T(1024)S(1)} %copy-done.50), kind=kOutput, calls=%fused_computation.22 | convolution fusion | flops 4302307328 | bytes 18878464 | tf_op jit(solution)/shard_map/dot_general | solution.py:24
  396.2 28.0 %attend_back.2 = (bf16[1024,512]{1,0:T(8,128)(2,1)}, bf16[2176,1024]{1,0:T(8,128)(2,1)}) custom-call(s32[16]{0:T(128)} %compare_select_fusion.1.first_ref, bf16[1024,1024]{1,0:T(8,128)(2,1)} %fusion.14.q_ref, bf16[2176,2048]{1,0:T(8,128)(2,1)} %add_convert_fusion.k_ref.v_ref, bf16[2176,2048]{1,0:T(8,128)(2,1)} %add_convert_fusion.k_ref.v_ref, ...), custom_call_target="tpu_custom_call" | custom-call | flops 31037849600 | bytes 8388608 | tf_op jit(solution)/shard_map/attend_back/pallas_call | solution.py:197
  431.6 19.8 %collective-permute-done.17 = bf16[1024,1024]{1,0:T(8,128)(2,1)} collective-permute-done((bf16[1024,1024]{1,0:T(8,128)(2,1)}, bf16[1024,1024]{1,0:T(8,128)(2,1)}, u32[]{:S(2)}, u32[]{:S(2)}) %collective-permute-start.17) | collective-permute-done | bytes 2097184 | tf_op jit(solution)/shard_map/ppermute | solution.py:298
  461.3 9.8 %collective-permute-start.18 = (bf16[512,1024]{1,0:T(8,128)(2,1)S(1)}, bf16[512,1024]{1,0:T(8,128)(2,1)}, u32[]{:S(2)}, u32[]{:S(2)}) collective-permute-start(bf16[512,1024]{1,0:T(8,128)(2,1)S(1)} %slice.616), channel_id=1, source_target_pairs={{0,2},{1,5},{2,0},{3,7},{4,6},{5,1},{6,4},{7,3},{8,10},{9,13},{10,... | collective-permute-start | bytes 3145736 | tf_op jit(solution)/shard_map/ppermute | solution.py:298
  475.1 13.5 %collective-permute-start.20 = (bf16[512,1536]{1,0:T(8,128)(2,1)}, bf16[512,1536]{1,0:T(8,128)(2,1)}, u32[]{:S(2)}, u32[]{:S(2)}) collective-permute-start(bf16[512,1536]{1,0:T(8,128)(2,1)} %pad_maximum_fusion.4), channel_id=1, source_target_pairs={{0,1},{1,0},{2,3},{3,2},{4,5},{5,4},{6,7},{7,6},{8,9},{9,8},{10,11... | collective-permute-start | bytes 4718600 | tf_op jit(solution)/shard_map/ppermute | solution.py:298
  488.6 27.6 %attend_back.3 = (bf16[1024,512]{1,0:T(8,128)(2,1)}, bf16[2176,1024]{1,0:T(8,128)(2,1)}) custom-call(s32[16]{0:T(128)} %compare_select_fusion.1.first_ref, bf16[1024,1024]{1,0:T(8,128)(2,1)} %fusion.14.q_ref, bf16[2176,2048]{1,0:T(8,128)(2,1)} %add_convert_fusion.k_ref.v_ref, bf16[2176,2048]{1,0:T(8,128)(2,1)} %add_convert_fusion.k_ref.v_ref, ...), custom_call_target="tpu_custom_call" | custom-call | flops 31037849600 | bytes 8388608 | tf_op jit(solution)/shard_map/attend_back/pallas_call | solution.py:197
  559.2 10.5 %collective-permute-start.35 = (bf16[128,1024]{1,0:T(8,128)(2,1)}, bf16[128,1024]{1,0:T(8,128)(2,1)}, u32[]{:S(2)}, u32[]{:S(2)}) collective-permute-start(bf16[128,1024]{1,0:T(8,128)(2,1)} %get-tuple-element.179), channel_id=1, source_target_pairs={{0,16},{1,17},{2,18},{3,19},{4,20},{5,21},{6,22},{7,23},{8,24},{9,... | collective-permute-start | bytes 786440 | tf_op jit(solution)/shard_map/ppermute | solution.py:298
  581.2 12.8 %collective-permute-done.35 = bf16[128,1024]{1,0:T(8,128)(2,1)} collective-permute-done((bf16[128,1024]{1,0:T(8,128)(2,1)}, bf16[128,1024]{1,0:T(8,128)(2,1)}, u32[]{:S(2)}, u32[]{:S(2)}) %collective-permute-start.35) | collective-permute-done | bytes 262176 | tf_op jit(solution)/shard_map/ppermute | solution.py:298
  597.9 18.5 %collective-permute-done.38 = bf16[128,1024]{1,0:T(8,128)(2,1)S(1)} collective-permute-done((bf16[128,1024]{1,0:T(8,128)(2,1)S(1)}, bf16[128,1024]{1,0:T(8,128)(2,1)S(1)}, u32[]{:S(2)}, u32[]{:S(2)}) %collective-permute-start.38) | collective-permute-done | bytes 262176 | tf_op jit(solution)/shard_map/ppermute | solution.py:298
  642.2 9.3 %copy.108 = f32[2176,1024]{0,1:T(8,128)} copy(f32[2176,1024]{1,0:T(8,128)} %fusion.17) | data formatting | bytes 17825792 | tf_op jit(solution)/shard_map/optimization_barrier | solution.py:527
  651.4 10.1 %fusion.15 = f32[2176,1024]{0,1:T(8,128)} fusion(bf16[2176,1024]{1,0:T(8,128)(2,1)} %get-tuple-element.82, bf16[1024,3200]{1,0:T(8,128)(2,1)} %all-gather.3.cloned.1.call-done), kind=kOutput, calls=%fused_computation.64 | convolution fusion | flops 4563402752 | bytes 15466496 | tf_op jit(solution)/shard_map/dot_general | solution.py:20
  661.6 11.5 %fusion.75 = (f32[1024]{0:T(1024)S(1)}, f32[1024]{0:T(1024)S(1)}, f32[2176,1024]{0,1:T(8,128)}, f32[2176,1024]{0,1:T(8,128)}) fusion(f32[2176]{0:T(1024)S(1)} %copy-done.33, f32[2176]{0:T(1024)S(1)} %copy-done.31, bf16[2176,1024]{0,1:T(8,128)(2,1)S(1)} %bitcast.51, f32[2176,1024]{0,1:T(8,128)} %copy.108, f32[2176,1024]{0,1:T(8,128)} %fusion.15), kind=kLoop, calls=%fused_computation.199 | loop fusion | flops 15595520 | bytes 40133632 | tf_op jit(solution)/shard_map/reduce_sum | solution.py:460
  730.8 133.5 %reduce-scatter.5.cloned.1.call-done = f32[32,128]{1,0:T(8,128)} async-done(((f32[1024,128]{1,0:T(8,128)}), f32[32,128]{1,0:T(8,128)}) %reduce-scatter.5.cloned.1.call-update) | async-done | bytes 16400 | tf_op jit(solution)/shard_map/reduce_scatter | solution.py:478
  (432 shorter events, 374.3 us)
Async XLA Ops:
  7.2 128.6 %all-gather.3.cloned.1.call-start = ((), (), s32[]{:S(2)}) async-start(), calls=%async_computation.2 | async-start | bytes 6758400 | tf_op jit(solution)/shard_map/all_gather | solution.py:375
  19.5 206.6 %all-gather.5.cloned.1.call-start = ((), (), s32[]{:S(2)}) async-start(), calls=%async_computation.3 | async-start | bytes 2162688 | tf_op jit(solution)/shard_map/all_gather | solution.py:384
  25.7 44.3 %collective-permute-start.7 = (bf16[128,1024]{1,0:T(8,128)(2,1)}, bf16[128,1024]{1,0:T(8,128)(2,1)}, u32[]{:S(2)}, u32[]{:S(2)}) collective-permute-start(bf16[128,1024]{1,0:T(8,128)(2,1)} %param.34), channel_id=1, source_target_pairs={{0,24},{1,25},{2,26},{3,27},{4,28},{5,29},{6,30},{7,31},{8,0},{9,1... | collective-permute-start | bytes 786440 | tf_op jit(solution)/shard_map/ppermute | solution.py:298
  28.5 51.1 %collective-permute-start.8 = (bf16[128,1024]{1,0:T(8,128)(2,1)}, bf16[128,1024]{1,0:T(8,128)(2,1)}, u32[]{:S(2)}, u32[]{:S(2)}) collective-permute-start(bf16[128,1024]{1,0:T(8,128)(2,1)} %param.34), channel_id=1, source_target_pairs={{0,16},{1,17},{2,18},{3,19},{4,20},{5,21},{6,22},{7,23},{8,24},{9,... | collective-permute-start | bytes 786440 | tf_op jit(solution)/shard_map/ppermute | solution.py:298
  29.7 513.6 %reduce-scatter.3.cloned.1.call-start = ((), (), s32[]{:S(2)}) async-start(), calls=%async_computation.4 | async-start | bytes 4325376 | tf_op jit(solution)/shard_map/reduce_scatter | solution.py:478
  37.1 42.6 %collective-permute-start.9 = (bf16[128,1024]{1,0:T(8,128)(2,1)}, bf16[128,1024]{1,0:T(8,128)(2,1)}, u32[]{:S(2)}, u32[]{:S(2)}) collective-permute-start(bf16[128,1024]{1,0:T(8,128)(2,1)} %param.34), channel_id=1, source_target_pairs={{0,8},{1,9},{2,10},{3,11},{4,12},{5,13},{6,14},{7,15},{8,16},{9,17... | collective-permute-start | bytes 786440 | tf_op jit(solution)/shard_map/ppermute | solution.py:298
  53.9 40.6 %collective-permute-start = (bf16[576,1024]{1,0:T(8,128)(2,1)S(1)}, bf16[576,1024]{1,0:T(8,128)(2,1)}, u32[]{:S(2)}, u32[]{:S(2)}) collective-permute-start(bf16[576,1024]{1,0:T(8,128)(2,1)S(1)} %get-tuple-element.174), channel_id=1, source_target_pairs={{0,1},{1,2},{2,3},{3,4},{4,5},{5,6},{6,7},{7,8},{8,9},{9,10},{10,1... | collective-permute-start | bytes 3538952 | tf_op jit(solution)/shard_map/ppermute | solution.py:272
  70.0 43.9 %collective-permute-start.5 = (bf16[512,1024]{1,0:T(8,128)(2,1)}, bf16[512,1024]{1,0:T(8,128)(2,1)}, u32[]{:S(2)}, u32[]{:S(2)}) collective-permute-start(bf16[512,1024]{1,0:T(8,128)(2,1)} %pad_maximum_fusion.6), channel_id=1, source_target_pairs={{0,2},{1,5},{2,0},{3,7},{4,6},{5,1},{6,4},{7,3},{8,10},{9,13},{10,... | collective-permute-start | bytes 3145736 | tf_op jit(solution)/shard_map/ppermute | solution.py:298
  81.9 51.3 %collective-permute-start.10 = (bf16[512,1024]{1,0:T(8,128)(2,1)}, bf16[512,1024]{1,0:T(8,128)(2,1)}, u32[]{:S(2)}, u32[]{:S(2)}) collective-permute-start(bf16[512,1024]{1,0:T(8,128)(2,1)} %pad_maximum_fusion.7), channel_id=1, source_target_pairs={{0,2},{1,5},{2,0},{3,7},{4,6},{5,1},{6,4},{7,3},{8,10},{9,13},{10,... | collective-permute-start | bytes 3145736 | tf_op jit(solution)/shard_map/ppermute | solution.py:298
  232.3 65.8 %collective-permute-start.13 = (bf16[2048,1024]{1,0:T(8,128)(2,1)}, bf16[2048,1024]{1,0:T(8,128)(2,1)}, u32[]{:S(2)}, u32[]{:S(2)}) collective-permute-start(bf16[2048,1024]{1,0:T(8,128)(2,1)} %get-tuple-element.58), channel_id=1, source_target_pairs={{0,1},{1,0},{2,3},{3,2},{4,5},{5,4},{6,7},{7,6},{8,9},{9,8},{10,11... | collective-permute-start | bytes 12582920 | tf_op jit(solution)/shard_map/ppermute | solution.py:298
  237.0 47.9 %collective-permute-start.12 = (bf16[2048,1024]{1,0:T(8,128)(2,1)}, bf16[2048,1024]{1,0:T(8,128)(2,1)}, u32[]{:S(2)}, u32[]{:S(2)}) collective-permute-start(bf16[2048,1024]{1,0:T(8,128)(2,1)} %get-tuple-element.57), channel_id=1, source_target_pairs={{0,1},{1,0},{2,3},{3,2},{4,5},{5,4},{6,7},{7,6},{8,9},{9,8},{10,11... | collective-permute-start | bytes 12582920 | tf_op jit(solution)/shard_map/ppermute | solution.py:298
  313.8 51.8 %collective-permute-start.14 = (bf16[2048,1024]{1,0:T(8,128)(2,1)}, bf16[2048,1024]{1,0:T(8,128)(2,1)}, u32[]{:S(2)}, u32[]{:S(2)}) collective-permute-start(bf16[2048,1024]{1,0:T(8,128)(2,1)} %convolution_convert_fusion.2), channel_id=1, source_target_pairs={{0,1},{1,0},{2,3},{3,2},{4,5},{5,4},{6,7},{7,6},{8,9},{9,8},{10,11... | collective-permute-start | bytes 12582920 | tf_op jit(solution)/shard_map/ppermute | solution.py:298
  314.5 62.4 %collective-permute-start.15 = (bf16[2048,1024]{1,0:T(8,128)(2,1)}, bf16[2048,1024]{1,0:T(8,128)(2,1)}, u32[]{:S(2)}, u32[]{:S(2)}) collective-permute-start(bf16[2048,1024]{1,0:T(8,128)(2,1)} %convolution_convert_fusion.1), channel_id=1, source_target_pairs={{0,1},{1,0},{2,3},{3,2},{4,5},{5,4},{6,7},{7,6},{8,9},{9,8},{10,11... | collective-permute-start | bytes 12582920 | tf_op jit(solution)/shard_map/ppermute | solution.py:298
  355.4 509.0 %reduce-scatter.5.cloned.1.call-start = ((), (), s32[]{:S(2)}) async-start(), calls=%async_computation.5 | async-start | bytes 540672 | tf_op jit(solution)/shard_map/reduce_scatter | solution.py:478
  394.1 57.2 %collective-permute-start.17 = (bf16[1024,1024]{1,0:T(8,128)(2,1)}, bf16[1024,1024]{1,0:T(8,128)(2,1)}, u32[]{:S(2)}, u32[]{:S(2)}) collective-permute-start(bf16[1024,1024]{1,0:T(8,128)(2,1)} %slice.613), channel_id=1, source_target_pairs={{0,4},{1,3},{2,6},{3,1},{4,0},{5,7},{6,2},{7,5},{8,12},{9,11},{10,... | collective-permute-start | bytes 6291464 | tf_op jit(solution)/shard_map/ppermute | solution.py:298
  461.3 82.0 %collective-permute-start.18 = (bf16[512,1024]{1,0:T(8,128)(2,1)S(1)}, bf16[512,1024]{1,0:T(8,128)(2,1)}, u32[]{:S(2)}, u32[]{:S(2)}) collective-permute-start(bf16[512,1024]{1,0:T(8,128)(2,1)S(1)} %slice.616), channel_id=1, source_target_pairs={{0,2},{1,5},{2,0},{3,7},{4,6},{5,1},{6,4},{7,3},{8,10},{9,13},{10,... | collective-permute-start | bytes 3145736 | tf_op jit(solution)/shard_map/ppermute | solution.py:298
  471.1 72.1 %collective-permute-start.19 = (bf16[512,1024]{1,0:T(8,128)(2,1)}, bf16[512,1024]{1,0:T(8,128)(2,1)}, u32[]{:S(2)}, u32[]{:S(2)}) collective-permute-start(bf16[512,1024]{1,0:T(8,128)(2,1)} %slice.615), channel_id=1, source_target_pairs={{0,2},{1,5},{2,0},{3,7},{4,6},{5,1},{6,4},{7,3},{8,10},{9,13},{10,... | collective-permute-start | bytes 3145736 | tf_op jit(solution)/shard_map/ppermute | solution.py:298
  475.1 68.2 %collective-permute-start.20 = (bf16[512,1536]{1,0:T(8,128)(2,1)}, bf16[512,1536]{1,0:T(8,128)(2,1)}, u32[]{:S(2)}, u32[]{:S(2)}) collective-permute-start(bf16[512,1536]{1,0:T(8,128)(2,1)} %pad_maximum_fusion.4), channel_id=1, source_target_pairs={{0,1},{1,0},{2,3},{3,2},{4,5},{5,4},{6,7},{7,6},{8,9},{9,8},{10,11... | collective-permute-start | bytes 4718600 | tf_op jit(solution)/shard_map/ppermute | solution.py:298
  555.8 62.6 %collective-permute-start.22 = (bf16[256,1536]{1,0:T(8,128)(2,1)}, bf16[256,1536]{1,0:T(8,128)(2,1)}, u32[]{:S(2)}, u32[]{:S(2)}) collective-permute-start(bf16[256,1536]{1,0:T(8,128)(2,1)} %slice.618), channel_id=1, source_target_pairs={{0,4},{1,3},{2,6},{3,1},{4,0},{5,7},{6,2},{7,5},{8,12},{9,11},{10,... | collective-permute-start | bytes 2359304 | tf_op jit(solution)/shard_map/ppermute | solution.py:298
  572.9 45.4 %collective-permute-start.21 = (bf16[512,1536]{1,0:T(8,128)(2,1)}, bf16[512,1536]{1,0:T(8,128)(2,1)}, u32[]{:S(2)}, u32[]{:S(2)}) collective-permute-start(bf16[512,1536]{1,0:T(8,128)(2,1)} %pad_maximum_fusion.5), channel_id=1, source_target_pairs={{0,1},{1,0},{2,3},{3,2},{4,5},{5,4},{6,7},{7,6},{8,9},{9,8},{10,11... | collective-permute-start | bytes 4718600 | tf_op jit(solution)/shard_map/ppermute | solution.py:298
  639.9 54.6 %collective-permute-start.25 = (bf16[128,1536]{1,0:T(8,128)(2,1)}, bf16[128,1536]{1,0:T(8,128)(2,1)S(1)}, u32[]{:S(2)}, u32[]{:S(2)}) collective-permute-start(bf16[128,1536]{1,0:T(8,128)(2,1)} %slice.619), channel_id=1, source_target_pairs={{0,2},{1,5},{2,0},{3,7},{4,6},{5,1},{6,4},{7,3},{8,10},{9,13},{10,... | collective-permute-start | bytes 1179656 | tf_op jit(solution)/shard_map/ppermute | solution.py:298
  639.9 49.2 %collective-permute-start.30 = (bf16[32,1536]{1,0:T(8,128)(2,1)}, bf16[32,1536]{1,0:T(8,128)(2,1)}, u32[]{:S(2)}, u32[]{:S(2)}) collective-permute-start(bf16[32,1536]{1,0:T(8,128)(2,1)} %get-tuple-element.194), channel_id=1, source_target_pairs={{0,24},{1,25},{2,26},{3,27},{4,28},{5,29},{6,30},{7,31},{8,0},{9,1... | collective-permute-start | bytes 294920 | tf_op jit(solution)/shard_map/ppermute | solution.py:298
  640.1 53.3 %collective-permute-start.29 = (bf16[32,1536]{1,0:T(8,128)(2,1)S(1)}, bf16[32,1536]{1,0:T(8,128)(2,1)}, u32[]{:S(2)}, u32[]{:S(2)}) collective-permute-start(bf16[32,1536]{1,0:T(8,128)(2,1)S(1)} %get-tuple-element.195), channel_id=1, source_target_pairs={{0,16},{1,17},{2,18},{3,19},{4,20},{5,21},{6,22},{7,23},{8,24},{9,... | collective-permute-start | bytes 294920 | tf_op jit(solution)/shard_map/ppermute | solution.py:298
  640.2 53.2 %collective-permute-start.28 = (bf16[32,1536]{1,0:T(8,128)(2,1)S(1)}, bf16[32,1536]{1,0:T(8,128)(2,1)}, u32[]{:S(2)}, u32[]{:S(2)}) collective-permute-start(bf16[32,1536]{1,0:T(8,128)(2,1)S(1)} %get-tuple-element.196), channel_id=1, source_target_pairs={{0,8},{1,9},{2,10},{3,11},{4,12},{5,13},{6,14},{7,15},{8,16},{9,17... | collective-permute-start | bytes 294920 | tf_op jit(solution)/shard_map/ppermute | solution.py:298
  (100 other events, 1419.7 us)
Sparse Core Ops, SparseCore 0:
  19.6 106.3 all-gather.2
  128.8 54.5 all-gather.4
  355.5 154.1 reduce-scatter.2
  719.9 144.4 reduce-scatter.4

commit v3 on v2

--- a/solution.py
+++ b/solution.py
@@ -53,17 +53,17 @@
 
 
 def attend_body(first_ref, q_ref, k_ref, v_ref, out_ref, lse_ref):
-    rows = q_ref.shape[0]
-    tiles = rows // TILE
+    tiles = out_ref.shape[0] // TILE
 
     def tile(j, carry):
         at = pl.multiple_of(j * TILE, TILE)
         here = pl.ds(at, TILE)
+        asking = pl.ds(pl.multiple_of(at + RIM, 64), TILE)
 
         def item(first, pair):
             lanes = slice(pair * 128, pair * 128 + 128)
             start, offset = key_window(first, k_ref.shape[0])
-            scores = dot_nt(k_ref[pl.ds(start, KEYS), lanes], paired(q_ref[here, lanes]))
+            scores = dot_nt(k_ref[pl.ds(start, KEYS), lanes], paired(q_ref[asking, lanes]))
             scores = keep_image(scores, offset)
             peak = jnp.max(scores, axis=0, keepdims=True)
             weights = jnp.exp(scores - peak)
@@ -100,16 +100,19 @@
 
 
 def attend_back_body(
-    first_ref, q_ref, k_ref, v_ref, grad_ref, lse_ref, dq_ref, dkv_ref, dk_sum, dv_sum
+    first_ref, q_ref, k_ref, v_ref, grad_ref, lse_ref, mixed_ref, dk_sum, dv_sum
 ):
-    rows = q_ref.shape[0]
+    rows = grad_ref.shape[0]
     tiles = rows // TILE
+    mixed_ref[:RIM, :LANES] = jnp.zeros((RIM, LANES), jnp.bfloat16)
+    mixed_ref[RIM + rows :, :LANES] = jnp.zeros((RIM, LANES), jnp.bfloat16)
     dk_sum[...] = jnp.zeros_like(dk_sum)
     dv_sum[...] = jnp.zeros_like(dv_sum)
 
     def tile(j, carry):
         at = pl.multiple_of(j * TILE, TILE)
         here = pl.ds(at, TILE)
+        asking = pl.ds(pl.multiple_of(at + RIM, 64), TILE)
         column = lax.broadcasted_iota(jnp.int32, (1, TILE), 1) + at
 
         def item(first, pair):
@@ -117,7 +120,7 @@
             start, offset = key_window(first, k_ref.shape[0])
             window = pl.ds(start, KEYS)
             keys = k_ref[window, lanes]
-            queries = paired(q_ref[here, lanes])
+            queries = paired(q_ref[asking, lanes])
             grads = paired(grad_ref[here, lanes])
             inside = (column >= first) & (column < first + IMG)
             lse = jnp.concatenate(
@@ -137,19 +140,19 @@
 
         one, two = first_ref[j], first_ref[tiles + j]
         for pair in range(LANES // 128):
-            dq_ref[here, pair * 128 : pair * 128 + 128] = item(one, pair)
+            mixed_ref[asking, pair * 128 : pair * 128 + 128] = item(one, pair)
 
         @pl.when(two != one)
         def _():
             for pair in range(LANES // 128):
                 lanes = slice(pair * 128, pair * 128 + 128)
-                dq_ref[here, lanes] = dq_ref[here, lanes] + item(two, pair)
+                mixed_ref[asking, lanes] = mixed_ref[asking, lanes] + item(two, pair)
 
         return carry
 
     lax.fori_loop(0, tiles, tile, 0)
-    dkv_ref[:, :LANES] = dk_sum[...].astype(jnp.bfloat16)
-    dkv_ref[:, LANES:] = dv_sum[...].astype(jnp.bfloat16)
+    mixed_ref[:, LANES : 2 * LANES] = dk_sum[...].astype(jnp.bfloat16)
+    mixed_ref[:, 2 * LANES :] = dv_sum[...].astype(jnp.bfloat16)
 
 
 def attention_cost(rows, width, products):
@@ -160,72 +163,129 @@
     )
 
 
-def attend(firsts, queries, key_vals):
-    rows, width = queries.shape
-    ext = key_vals.shape[0]
-    groups = width // LANES
+def mixed_specs(ext, base):
+    return [
+        pl.BlockSpec((ext, LANES), lambda g, f, at=at: (0, 3 * (base + g) + at)) for at in range(3)
+    ]
+
+
+def attend(firsts, mixed, rows, part):
+    ext, width = mixed.shape[0], mixed.shape[1] // 3
+    groups = width // LANES // 2
     return pl.pallas_call(
         attend_body,
         grid_spec=pltpu.PrefetchScalarGridSpec(
             num_scalar_prefetch=1,
             grid=(groups,),
-            in_specs=[
-                pl.BlockSpec((rows, LANES), lambda g, f: (0, g)),
-                pl.BlockSpec((ext, LANES), lambda g, f: (0, 2 * g)),
-                pl.BlockSpec((ext, LANES), lambda g, f: (0, 2 * g + 1)),
-            ],
+            in_specs=mixed_specs(ext, part * groups),
             out_specs=[
                 pl.BlockSpec((rows, LANES), lambda g, f: (0, g)),
                 pl.BlockSpec((1, LANES // HEAD_DIM, rows), lambda g, f: (g, 0, 0)),
             ],
         ),
         out_shape=[
-            jax.ShapeDtypeStruct((rows, width), jnp.bfloat16),
+            jax.ShapeDtypeStruct((rows, width // 2), jnp.bfloat16),
             jax.ShapeDtypeStruct((groups, LANES // HEAD_DIM, rows), jnp.float32),
         ],
-        cost_estimate=attention_cost(rows, width, 2),
+        cost_estimate=attention_cost(rows, width // 2, 3),
         name="attend",
-    )(firsts, queries, key_vals, key_vals)
-
-
-def attend_back(firsts, queries, key_vals, grads, lse, part):
-    rows, width = queries.shape
-    ext = key_vals.shape[0]
+    )(firsts, mixed, mixed, mixed)
+
+
+def attend_back(firsts, mixed, grads, lse, part):
+    ext, width = mixed.shape[0], mixed.shape[1] // 3
+    rows = grads.shape[0]
     groups = width // LANES // 2
     base = part * groups
-    own = pl.BlockSpec((rows, LANES), lambda g, f: (0, base + g))
     return pl.pallas_call(
         attend_back_body,
         grid_spec=pltpu.PrefetchScalarGridSpec(
             num_scalar_prefetch=1,
             grid=(groups,),
-            in_specs=[
-                own,
-                pl.BlockSpec((ext, LANES), lambda g, f: (0, 2 * (base + g))),
-                pl.BlockSpec((ext, LANES), lambda g, f: (0, 2 * (base + g) + 1)),
-                own,
-                pl.BlockSpec((1, LANES // HEAD_DIM, rows), lambda g, f: (base + g, 0, 0)),
+            in_specs=mixed_specs(ext, base)
+            + [
+                pl.BlockSpec((rows, LANES), lambda g, f: (0, base + g)),
+                pl.BlockSpec((1, LANES // HEAD_DIM, rows), lambda g, f: (g, 0, 0)),
             ],
-            out_specs=[
-                pl.BlockSpec((rows, LANES), lambda g, f: (0, g)),
-                pl.BlockSpec((ext, 2 * LANES), lambda g, f: (0, g)),
-            ],
+            out_specs=pl.BlockSpec((ext, 3 * LANES), lambda g, f: (0, g)),
             scratch_shapes=[pltpu.VMEM((ext, LANES), jnp.float32)] * 2,
         ),
-        out_shape=[
-            jax.ShapeDtypeStruct((rows, width // 2), jnp.bfloat16),
-            jax.ShapeDtypeStruct((ext, width), jnp.bfloat16),
-        ],
+        out_shape=jax.ShapeDtypeStruct((ext, 3 * width // 2), jnp.bfloat16),
         cost_estimate=attention_cost(rows, width // 2, 5),
         name="attend_back",
-    )(firsts, queries, key_vals, key_vals, grads, lse)
-
-
-def by_group(keys, values):
+    )(firsts, mixed, mixed, mixed, grads, lse)
+
+
+def into_norm_body(first_ref, second_ref, w_ref, tokens_ref, out_ref, sums_ref, mixed_sums_ref):
+    cut = first_ref.shape[1]
+    grads = dot_nt(first_ref[...], w_ref[:, :cut]) + dot_nt(
+        second_ref[...], w_ref[:, cut : 2 * cut]
+    )
+    out_ref[...] = grads.astype(jnp.bfloat16)
+    unit = normed_parts(tokens_ref[...].astype(jnp.float32))[0]
+    lines = jnp.concatenate(
+        [jnp.sum(grads * unit, axis=0, keepdims=True), jnp.sum(grads, axis=0, keepdims=True)],
+        axis=0,
+    )
+    sides = [
+        jnp.sum(ref[...].astype(jnp.float32), axis=0, keepdims=True)
+        for ref in (first_ref, second_ref)
+    ]
+
+    @pl.when(pl.program_id(0) == 0)
+    def _():
+        sums_ref[...] = jnp.zeros_like(sums_ref)
+        mixed_sums_ref[...] = jnp.zeros_like(mixed_sums_ref)
+
+    sums_ref[...] += lines
+    mixed_sums_ref[:, :cut] += sides[0]
+    mixed_sums_ref[:, cut:] += sides[1]
+
+
+def into_norm(first, second, w_mixed, tokens):
+    ext, cut = first.shape
+    width = tokens.shape[1]
+    steps = 4
+    block = ext // steps
+    whole = lambda i: (0, 0)
+    return pl.pallas_call(
+        into_norm_body,
+        grid=(steps,),
+        in_specs=[
+            pl.BlockSpec((block, cut), lambda i: (i, 0)),
+            pl.BlockSpec((block, cut), lambda i: (i, 0)),
+            pl.BlockSpec(w_mixed.shape, whole, pipeline_mode=pl.Buffered(1)),
+            pl.BlockSpec((block, width), lambda i: (i, 0)),
+        ],
+        out_specs=[
+            pl.BlockSpec((block, width), lambda i: (i, 0)),
+            pl.BlockSpec((2, width), whole),
+            pl.BlockSpec((1, 2 * cut), whole),
+        ],
+        out_shape=[
+            jax.ShapeDtypeStruct((ext, width), jnp.bfloat16),
+            jax.ShapeDtypeStruct((2, width), jnp.float32),
+            jax.ShapeDtypeStruct((1, 2 * cut), jnp.float32),
+        ],
+        cost_estimate=pl.CostEstimate(
+            flops=4 * ext * cut * width, bytes_accessed=8 * ext * cut, transcendentals=0
+        ),
+        name="into_norm",
+    )(first, second, w_mixed, tokens)
+
+
+def grouped(queries, keys, values):
     parts = []
     for at in range(0, keys.shape[-1], LANES):
-        parts += [keys[..., at : at + LANES], values[..., at : at + LANES]]
+        parts += [part[..., at : at + LANES] for part in (queries, keys, values)]
     return parts
+
+
+def ungrouped(columns, which):
+    width = columns.shape[-1]
+    return [
+        columns[..., at : at + LANES] for at in range(which * LANES, width, 3 * LANES)
+    ]
 
 
 def image_firsts(padding, ident):
@@ -303,6 +363,9 @@
     def pair(self, value, stage):
         return self.permute(value, lambda i: i ^ (1 << self.orders[i & 1][stage]))
 
+    def pairs(self, values, stage):
+        return [self.pair(value, stage) for value in values]
+
     def swap(self, value):
         return self.permute(value, lambda i: i ^ 1)
 
@@ -319,23 +382,36 @@
     def quad(self, block):
         return jnp.concatenate([block] + [self.turn(block, -r) for r in (1, 2, 3)], axis=0)
 
-    def cut(self, total):
-        at = total.shape[0] // 2
-        return total[:at], total[at:].astype(jnp.bfloat16)
-
-    def quarters(self, total):
-        rows = total.shape[0] // 4
-        sent = [total[r * rows : (r + 1) * rows].astype(jnp.bfloat16) for r in (1, 2, 3)]
-        return total[:rows], sent
+    def cut(self, totals):
+        at = totals[0].shape[0] // 2
+        sent = [total[at:].astype(jnp.bfloat16) for total in totals]
+        return [total[:at] for total in totals], sent
+
+    def quarters(self, totals):
+        rows = totals[0].shape[0] // 4
+        sent = []
+        for r in (1, 2, 3):
+            here = slice(r * rows, (r + 1) * rows)
+            sent.append(jnp.concatenate([t[here].astype(jnp.bfloat16) for t in totals], axis=1))
+        return [total[:rows] for total in totals], sent
 
     def turned(self, parts):
         return [self.turn(part, r) for r, part in zip((1, 2, 3), parts)]
 
 
-def added(kept, *received):
-    for part in received:
-        kept = kept + part.astype(jnp.float32)
-    return kept
+def added(kept, received):
+    return [total + part.astype(jnp.float32) for total, part in zip(kept, received)]
+
+
+def quarters_added(kept, received):
+    sums = []
+    at = 0
+    for total in kept:
+        for part in received:
+            total = total + part[:, at : at + total.shape[1]].astype(jnp.float32)
+        sums.append(total)
+        at += total.shape[1]
+    return sums
 
 
 def after(value, *others):
@@ -372,23 +448,12 @@
     owners = rings.owners()
     side = jnp.concatenate(smalls)
     side = jnp.pad(side, (0, feat_rows * extra - side.shape[0])).reshape(feat_rows, extra)
-    qkv_side = lax.all_gather(
-        jnp.concatenate(
-            [w_qkv[:, :width]]
-            + by_group(w_qkv[:, width : 2 * width], w_qkv[:, 2 * width :])
-            + [side],
-            axis=1,
-        ),
-        "dev", axis=0, tiled=True
+    columns = grouped(w_qkv[:, :width], w_qkv[:, width : 2 * width], w_qkv[:, 2 * width :])
+    w_mixed = lax.all_gather(
+        jnp.concatenate(columns + [side], axis=1), "dev", axis=0, tiled=True
     )
     full_out = lax.all_gather(w_out, "dev", axis=0, tiled=True)
-    halves = [rings.quad(w_fc), rings.quad(w_proj)]
-    last = rings.stages - 1
-    for stage in range(last):
-        halves = [jnp.concatenate([h, rings.pair(h, stage)], axis=0) for h in halves]
-    halves = [(h, rings.pair(h, last)) for h in halves]
-    full_qkv = qkv_side[:, : 3 * width]
-    side_all = qkv_side[:, 3 * width :].reshape(size, feat_rows * extra).astype(wide)
+    side_all = w_mixed[:, 3 * width :].reshape(size, feat_rows * extra).astype(wide)
     vectors = []
     place = 0
     for small in smalls:
@@ -405,22 +470,39 @@
     )
     unit_one, scale_one = normed_parts(ext_tokens.astype(wide))
     normed_one = (unit_one * gain_one + bias_one).astype(low)
-    normed_own = normed_one[RIM : RIM + rows]
-    queries = (
-        (dot_nn(normed_own, full_qkv[:, :width]) + bias_qv[:width]).astype(low)
-        * HEAD_DIM**-0.5
-    ).astype(low)
-    kv_bias = jnp.concatenate(by_group(jnp.zeros((width,), wide), bias_qv[width:]))
-    key_vals = (dot_nn(normed_one, full_qkv[:, width:]) + kv_bias).astype(low)
+    none = jnp.zeros((width,), wide)
+    bias_mixed = jnp.concatenate(grouped(bias_qv[:width], none, bias_qv[width:]))
+    scale_mixed = jnp.concatenate(grouped(none + HEAD_DIM**-0.5, none + 1.0, none + 1.0))
+
+    last = rings.stages - 1
+    part_fc = rings.quad(after(w_fc, w_mixed))
+    part_proj = rings.quad(after(w_proj, w_mixed))
+    mixed = ((dot_nn(normed_one, w_mixed[:, : 3 * width]) + bias_mixed) * scale_mixed).astype(low)
+    mixed, part_fc = lax.optimization_barrier((mixed, part_fc))
+    for stage in range(last - 1):
+        part_fc = jnp.concatenate([part_fc, rings.pair(part_fc, stage)], axis=0)
+    pair_fc = rings.pair(part_fc, last - 1)
+    first_heads, first_lse = attend(firsts, mixed, rows, 0)
+    first_heads, pair_fc, part_proj = lax.optimization_barrier((first_heads, pair_fc, part_proj))
+    part_fc = jnp.concatenate([part_fc, pair_fc], axis=0)
+    for stage in range(last - 1):
+        part_proj = jnp.concatenate([part_proj, rings.pair(part_proj, stage)], axis=0)
+    mixed, part_fc, part_proj, full_out = lax.optimization_barrier(
+        (mixed, part_fc, part_proj, full_out)
+    )
+    pair_fc, pair_proj = rings.pair(part_fc, last), rings.pair(part_proj, last - 1)
+    second_heads, second_lse = attend(firsts, mixed, rows, 1)
+    second_heads, pair_fc, pair_proj = lax.optimization_barrier((second_heads, pair_fc, pair_proj))
+    fc_own = jnp.concatenate([part_fc, pair_fc], axis=0)
+    part_proj = jnp.concatenate([part_proj, pair_proj], axis=0)
+    second_heads, fc_own, part_proj = lax.optimization_barrier((second_heads, fc_own, part_proj))
+    fc_other = rings.swap(fc_own)
+    proj_own = jnp.concatenate([part_proj, rings.pair(part_proj, last)], axis=0)
+    proj_other = rings.swap(proj_own)
     feature = jnp.arange(width, dtype=jnp.int32)
     wanted = (owners[:, None] * feat_rows + jnp.arange(feat_rows, dtype=jnp.int32)).reshape(-1)
     reorder = (feature[:, None] == wanted[None, :]).astype(low)
-    normed_turned = dot_nn(normed_one, reorder).astype(low)
-    key_vals, halves = lax.optimization_barrier((key_vals, halves))
-    halves = [jnp.concatenate(h, axis=0) for h in halves]
-    queries, halves = lax.optimization_barrier((queries, halves))
-    (fc_own, proj_own), (fc_other, proj_other) = halves, [rings.swap(h) for h in halves]
-    attended, lse = attend(firsts, queries, key_vals)
+    attended = jnp.concatenate([first_heads, second_heads], axis=1)
 
     middle = tokens.astype(wide) + (dot_nn(attended, full_out) + bias_out)
     unit_two, scale_two = normed_parts(middle)
@@ -439,18 +521,25 @@
 
     gelu_own, pull_own = up(fc_own, proj_own, bias_fc[:half])
     gelu_other, pull_other = up(fc_other, proj_other, bias_fc[half:])
-    proj_sent = rings.swap(dot_tn(gelu_other, grad_result_low).astype(low))
-    proj_kept = dot_tn(gelu_own, grad_result_low)
     grad_hidden_own = down(pull_own, proj_own)
     grad_hidden_other = down(pull_other, proj_other)
-    fc_sent = rings.swap(dot_tn(grad_hidden_other, normed_two).astype(low))
-    fc_kept = dot_tn(grad_hidden_own, normed_two)
-    proj_kept, proj_cut = rings.cut(added(proj_kept, proj_sent))
-    proj_sent = rings.pair(proj_cut, last)
+    mlp_cut = [
+        dot_tn(grad_hidden_other, normed_two).astype(low),
+        dot_tn(gelu_other, grad_result_low).astype(low),
+    ]
+    mlp_sent = [rings.swap(part) for part in mlp_cut]
+    gelu_own = after(gelu_own, mlp_cut)
     up_own, up_other = dot_nn(gelu_own, proj_own), dot_nn(gelu_other, proj_other)
     output = (keep * (middle + up_own + up_other + bias_proj)).astype(low)
+    gelu_own, mlp_sent, output = lax.optimization_barrier((gelu_own, mlp_sent, output))
+    mlp_kept = added(
+        [dot_tn(grad_hidden_own, normed_two), dot_tn(gelu_own, grad_result_low)], mlp_sent
+    )
+    mlp_kept, mlp_cut = rings.cut(mlp_kept)
+    mlp_sent = rings.pairs(mlp_cut, last)
+    grad_hidden_own = after(grad_hidden_own, mlp_cut)
+    normed_turned = dot_nn(normed_one, reorder).astype(low)
     down_own, down_other = dot_nn(grad_hidden_own, fc_own), dot_nn(grad_hidden_other, fc_other)
-    fc_kept, fc_cut = rings.cut(added(fc_kept, fc_sent))
     grad_norm_two = down_own + down_other
     grad_middle = grad_result + norm_back(unit_two, scale_two, gain_two, grad_norm_two)
     grad_branch = grad_middle.astype(low)
@@ -461,11 +550,6 @@
 
     hidden_sums = jnp.concatenate([total(grad_hidden_own), total(grad_hidden_other)])
     hidden_sums = jnp.sum(jnp.where(chosen, hidden_sums.reshape(size, 1, -1), 0.0), axis=0)
-    def sided(vectors):
-        lines = jnp.concatenate([g.reshape(size, -1) for g in vectors], axis=1)
-        lines = jnp.pad(lines, ((0, 0), (0, feat_rows * extra - lines.shape[1])))
-        return lines.reshape(width, extra)
-
     def unsided(flat, vectors):
         parts = []
         at = 0
@@ -477,102 +561,94 @@
     def scattered(values):
         return lax.psum_scatter(values, "dev", scatter_dimension=0, tiled=True)
 
-    turned_own = normed_turned[RIM : RIM + rows]
     near, far = slice(0, width // 2), slice(width // 2, width)
 
-    def products(lines, grad_q, grad_kv):
-        return jnp.concatenate(
-            [dot_tn(turned_own[:, lines], grad_q), dot_tn(normed_turned[:, lines], grad_kv)], axis=1
-        )
+    def product(lines, grads):
+        return dot_tn(normed_turned[:, lines], grads)
 
     out_product = dot_tn(attended, grad_branch)
-    grad_attended = after(grad_attended, output, fc_cut, proj_cut, out_product)
-    fc_sent = rings.pair(fc_cut, last)
+    grad_attended, mlp_sent = lax.optimization_barrier((grad_attended, mlp_sent))
+    for stage in reversed(range(last)):
+        mlp_kept, mlp_cut = rings.cut(added(mlp_kept, mlp_sent))
+        mlp_sent = rings.pairs(mlp_cut, stage)
+    grad_attended = after(grad_attended, mlp_cut, out_product, normed_turned)
     grad_out = scattered(out_product)
-    first_q, first_kv = attend_back(firsts, queries, key_vals, grad_attended, lse, 0)
-
-    first_kv, fc_sent, proj_sent = lax.optimization_barrier((first_kv, fc_sent, proj_sent))
-    for stage in reversed(range(last)):
-        fc_kept, fc_cut = rings.cut(added(fc_kept, fc_sent))
-        proj_kept, proj_cut = rings.cut(added(proj_kept, proj_sent))
-        fc_sent, proj_sent = rings.pair(fc_cut, stage), rings.pair(proj_cut, stage)
-    first_cut = products(far, first_q, first_kv).astype(low)
-    first_sent = rings.swap(first_cut)
-    first_kept = products(near, first_q, first_kv)
-    grad_attended = after(grad_attended, first_kept, first_cut, fc_cut, proj_cut)
-    second_q, second_kv = attend_back(firsts, queries, key_vals, grad_attended, lse, 1)
-
-    second_kv, fc_sent, proj_sent, first_sent, grad_out = lax.optimization_barrier(
-        (second_kv, fc_sent, proj_sent, first_sent, grad_out)
-    )
-    fc_kept, fc_cut = rings.quarters(added(fc_kept, fc_sent))
-    proj_kept, proj_cut = rings.quarters(added(proj_kept, proj_sent))
+    first = attend_back(firsts, mixed, grad_attended, first_lse, 0)
+
+    first, mlp_sent = lax.optimization_barrier((first, mlp_sent))
+    mlp_kept, mlp_cut = rings.quarters(added(mlp_kept, mlp_sent))
+    mlp_sent = rings.turned(mlp_cut)
+    first_cut = product(far, after(first, mlp_cut)).astype(low)
+    first_sent = [rings.swap(first_cut)]
+    first_kept = [product(near, after(first, first_cut))]
+    grad_attended, first_kept = lax.optimization_barrier((grad_attended, first_kept))
+    second = attend_back(firsts, mixed, grad_attended, second_lse, 1)
+
+    second, first_sent, mlp_sent = lax.optimization_barrier((second, first_sent, mlp_sent))
     first_kept, first_cut = rings.cut(added(first_kept, first_sent))
-    first_sent = rings.pair(first_cut, last)
-    fc_sent, proj_sent = rings.turned(fc_cut), rings.turned(proj_cut)
-    second_kv = after(second_kv, fc_cut, proj_cut, first_cut)
-    second_cut = products(far, second_q, second_kv).astype(low)
-    second_sent = rings.swap(second_cut)
-    second_kept = products(near, second_q, after(second_kv, second_cut))
+    first_sent = rings.pairs(first_cut, last)
+    second_cut = product(far, after(second, first_cut)).astype(low)
+    second_sent = [rings.swap(second_cut)]
+    second_kept = [product(near, after(second, second_cut))]
     second_sent, first_sent, second_kept = lax.optimization_barrier(
         (second_sent, first_sent, second_kept)
     )
     second_kept, second_cut = rings.cut(added(second_kept, second_sent))
-    second_sent = rings.pair(second_cut, last)
+    second_sent = rings.pairs(second_cut, last)
     for stage in reversed(range(last)):
         first_kept, first_cut = rings.cut(added(first_kept, first_sent))
-        first_sent = rings.pair(first_cut, stage)
-    w_kv = full_qkv[:, width:]
-    grad_ext = dot_nt(after(first_kv, second_cut, first_cut), w_kv[:, :width])
-    grad_ext, first_sent, second_sent = lax.optimization_barrier((grad_ext, first_sent, second_sent))
+        first_sent = rings.pairs(first_cut, stage)
+    grad_ext, norm_sums, mixed_sums = into_norm(
+        first, after(second, second_cut, first_cut), w_mixed, ext_tokens
+    )
+    head = shifted(grad_ext[rows + RIM :], 1).astype(wide)
+    tail = shifted(grad_ext[:RIM], -1).astype(wide)
+    grad_ext, first_sent, second_sent, mlp_sent, grad_out = lax.optimization_barrier(
+        (grad_ext, first_sent, second_sent, mlp_sent, grad_out)
+    )
     for stage in reversed(range(last)):
         second_kept, second_cut = rings.cut(added(second_kept, second_sent))
-        second_sent = rings.pair(second_cut, stage)
+        second_sent = rings.pairs(second_cut, stage)
     first_kept, first_cut = rings.quarters(added(first_kept, first_sent))
     first_sent = rings.turned(first_cut)
-    grad_ext = grad_ext + dot_nt(after(second_kv, second_cut, first_cut), w_kv[:, width:])
-    grad_q = jnp.concatenate([first_q, second_q], axis=1)
-    grad_by_q = dot_nt(grad_q, full_qkv[:, :width])
-    grad_own = grad_ext[RIM : RIM + rows] + grad_by_q
-    head = shifted(grad_ext[rows + RIM :].astype(low), 1).astype(wide)
-    tail = shifted(grad_ext[:RIM].astype(low), -1).astype(wide)
-    grad_own, second_sent = lax.optimization_barrier((grad_own, second_sent))
+    grad_fc, grad_proj = quarters_added(mlp_kept, mlp_sent)
+    grad_own, grad_fc, grad_proj, second_sent = lax.optimization_barrier(
+        (after(grad_ext, second_cut, first_cut)[RIM : RIM + rows], grad_fc, grad_proj, second_sent)
+    )
     second_kept, second_cut = rings.quarters(added(second_kept, second_sent))
     second_sent = rings.turned(second_cut)
     grad_norm_one = (
-        grad_own
+        after(grad_own, second_cut).astype(wide)
         + jnp.pad(head, ((0, rows - RIM), (0, 0)))
         + jnp.pad(tail, ((rows - RIM, 0), (0, 0)))
     )
-    unit_own = unit_one[RIM : RIM + rows]
-    scale_own = scale_one[RIM : RIM + rows]
+    unit_own, scale_own = normed_parts(tokens.astype(wide))
     grad_tokens = (grad_middle + norm_back(unit_own, scale_own, gain_one, grad_norm_one)).astype(low)
 
-    grad_fc, grad_proj = added(fc_kept, *fc_sent), added(proj_kept, *proj_sent)
-    grad_first, grad_second = added(first_kept, *first_sent), added(second_kept, *second_sent)
-    value_sums = [total(first_kv).reshape(-1, 2, LANES), total(second_kv).reshape(-1, 2, LANES)]
-    value_sums = jnp.concatenate(value_sums, axis=0)[:, 1].reshape(-1)
-    side_grads = scattered(
-        sided(
-            (
-                total(grad_ext * unit_one) + total(grad_by_q * unit_own),
-                total(grad_ext) + total(grad_by_q),
-                jnp.concatenate([total(grad_q), value_sums]),
+    (grad_first,) = quarters_added(first_kept, first_sent)
+    (grad_second,) = quarters_added(second_kept, second_sent)
+    small_sums = jnp.concatenate(
+        [
+            g.reshape(size, -1)
+            for g in (
+                norm_sums[0],
+                norm_sums[1],
+                jnp.concatenate(ungrouped(mixed_sums[0], 0) + ungrouped(mixed_sums[0], 2)),
                 total(grad_branch),
                 total(grad_norm_two * unit_two),
                 total(grad_norm_two),
                 hidden_sums,
                 total(grad_result),
             )
-        )
-    )
-    small_outs = unsided(side_grads.reshape(-1), smalls)
-    both = (grad_first, grad_second)
-    columns = [part[:, : width // 2] for part in both]
-    for which in range(2):
-        for part in both:
-            for at in range(width // 2, part.shape[1], 2 * LANES):
-                columns.append(part[:, at + which * LANES : at + which * LANES + LANES])
+        ],
+        axis=1,
+    )
+    count = small_sums.shape[1]
+    all_sums = lax.all_gather(small_sums.reshape(1, size * count), "dev", axis=0, tiled=True)
+    own_sums = lax.dynamic_slice_in_dim(all_sums, lax.axis_index("dev") * count, count, axis=1)
+    small_outs = unsided(jnp.sum(own_sums, axis=0), smalls)
+    grad_mixed = jnp.concatenate([grad_first, grad_second], axis=1)
+    columns = [part for which in range(3) for part in ungrouped(grad_mixed, which)]
     return (
         output,
         grad_tokens,

time: 888 us -> 700 us (0.79)
  waiting for transfers between devices: 252 us -> 154 us
  matrix products: 209 us -> 168 us
  other arithmetic: 97.9 us -> 63.8 us
  Pallas kernels: 102 us -> 131 us
  starting transfers between devices: 82 us -> 55.3 us
  local copies, waits for them, and re-layouts: 117 us -> 106 us
    reduce_scatter x2 -> x1, waiting for transfers between devices: 134 us -> 0.02 us  [scattered(): return lax.psum_scatter(values, 'dev', scatter_dimension=0, tiled=True)]
    all_gather x1 -> x2, waiting for transfers between devices: 0.01 us -> 78 us  [the longest x1 63 us: shards(): lax.all_gather(jnp.concatenate(columns + [side], axis=1), 'dev', axis=0,...]
    ppermute x36 -> x33, waiting for transfers between devices: 118 us -> 75.5 us  [permute(): lax.ppermute(value, 'dev', [(i, target(i)) for i in range(self.size)])]
    ppermute x36 -> x33, starting transfers between devices: 72.5 us -> 46.8 us  [permute(): lax.ppermute(value, 'dev', [(i, target(i)) for i in range(self.size)])]
    dot_general x8 -> x5, matrix products: 67.4 us -> 42.9 us  [dot_nt(): lax.dot_general(a, b, (((1,), (1,)), ((), ())), preferred_element_type=jn...]
    pallas_call x0 -> x1, Pallas kernels: none -> 22.7 us  [into_norm(): pl.pallas_call(into_norm_body, grid=(steps,), in_specs=[pl.BlockSpec((blo...]
    reduce_sum x6 -> x2, other arithmetic: 24.6 us -> 5.1 us  [total(): return jnp.sum(values.astype(wide), axis=0)]
    concatenate x8 -> x14, local copies, waits for them, and re-layouts: 6.31 us -> 18.6 us  [the longest x9 15.5 us: shards(): jnp.concatenate(ungrouped(mixed_sums[0], 0) + ungrouped(mixed_sums[0], 2))]
  transfers between devices with their start and end apart: 44 -> 41, of which waited for: 14 -> 11; matrix products, arithmetic and copies ran while one was open for 40% -> 40% of each run, Pallas kernels for 12% -> 19%
where the time goes in v3:
time: 700 us; the launch traced here: 693 us
  matrix products  168 us (24%)
  waiting for transfers between devices  154 us (22%)
  Pallas kernels  131 us (19%)
  local copies, waits for them, and re-layouts  106 us (15%)
  other arithmetic  63.8 us (9%)
  starting transfers between devices  55.3 us (8%)
  between operations  15.4 us (2%)
    ppermute x33, waiting for transfers between devices, permute(): lax.ppermute(value, 'dev', [(i, target(i)) for i in range(self.size)])  75.5 us
    dot_general x7, matrix products, dot_nn(): lax.dot_general(a, b, (((1,), (0,)), ((), ())), preferred_element_type=jn...  65.2 us
    all_gather x1, waiting for transfers between devices, shards(): lax.all_gather(jnp.concatenate(columns + [side], axis=1), 'dev', axis=0,...  63 us
    dot_general x9, matrix products, dot_tn(): lax.dot_general(a, b, (((0,), (0,)), ((), ())), preferred_element_type=jn...  60.2 us
    pallas_call x2, Pallas kernels, attend_back(): pl.pallas_call(attend_back_body, grid_spec=pltpu.PrefetchScalarGridSpec(n...  57.7 us
    pallas_call x2, Pallas kernels, attend(): pl.pallas_call(attend_body, grid_spec=pltpu.PrefetchScalarGridSpec(num_sc...  50.7 us
    unnamed x187, local copies, waits for them, and re-layouts  47.5 us
    ppermute x33, starting transfers between devices, permute(): lax.ppermute(value, 'dev', [(i, target(i)) for i in range(self.size)])  46.8 us
  transfers between devices with their start and end apart: 41, of which 11 were waited for; matrix products, arithmetic and copies ran while one was open for 40% of the time, Pallas kernels for 19%

profile of v3, /device:TPU:0, one launch (start us, length us, event | category | flops | bytes accessed | tf_op | source)
XLA Modules:
  0.0 693.2 jit_solution(17934052428860624323)
XLA Ops:
  37.7 63.0 %all-gather.5.cloned.1.call-done.w_ref = bf16[1024,3200]{1,0:T(8,128)(2,1)} async-done(((bf16[32,3200]{1,0:T(8,128)(2,1)}), bf16[1024,3200]{1,0:T(8,128)(2,1)}) %all-gather.5.cloned.1.call-update) | async-done | bytes 6553616 | tf_op jit(solution)/shard_map/all_gather | solution.py:452
  132.0 21.8 %multiply_convert_fusion.q_ref.k_ref.v_ref = bf16[2176,3072]{1,0:T(8,128)(2,1)} fusion(f32[3072]{0:T(1024)} %constant.65.clone.1, f32[3072]{0:T(1024)} %constant_dynamic-update-slice_fusion.35, bf16[1024,3200]{1,0:T(8,128)(2,1)} %all-gather.5.cloned.1.call-done.w_ref, bf16[2176,1024]{1,0:T(8,128)(2,1)} %copy-done.3, f32[1024]{0:T(1024)S(1)} %add.244, ...), kind=kOutput, calls=%fused_computation | convolution fusion | flops 13723631616 | bytes 24167424 | tf_op jit(solution)/shard_map/dot_general | solution.py:28
  159.8 25.2 %attend.2 = (bf16[1024,512]{1,0:T(8,128)(2,1)}, f32[2,4,1024]{2,1,0:T(4,128)}) custom-call(s32[16]{0:T(128)} %compare_select_fusion.1.first_ref, bf16[2176,3072]{1,0:T(8,128)(2,1)} %multiply_convert_fusion.q_ref.k_ref.v_ref, bf16[2176,3072]{1,0:T(8,128)(2,1)} %multiply_convert_fusion.q_ref.k_ref.v_ref, bf16[2176,3072]{1,0:T(8,128)(2,1)} %multiply_convert_fusion.q_ref.k_ref.v_ref), custom_call_target="tpu_custom_call" | custom-call | flops 18622709760 | bytes 8388608 | tf_op jit(solution)/shard_map/attend/pallas_call | solution.py:175
  188.1 9.7 %convolution_convert_fusion = bf16[2176,1024]{1,0:T(8,128)(2,1)} fusion(s32[1024]{0:T(1024)S(1)} %copy-done.54, bf16[2176,1024]{1,0:T(8,128)(2,1)} %copy-done.3, f32[1024]{0:T(1024)S(1)} %add.244, f32[1024]{0:T(1024)S(1)} %mul.189, f32[2176]{0:T(1024)S(1)} %add_rsqrt_fusion, f32[2176]{0:T(1024)S(1)} %broadcast_multiply_fusion), kind=kOutput, calls=%fused_computation.31 | convolution fusion | flops 4580048896 | bytes 8942592 | tf_op jit(solution)/shard_map/dot_general | solution.py:28
  199.8 25.5 %attend.3 = (bf16[1024,512]{1,0:T(8,128)(2,1)}, f32[2,4,1024]{2,1,0:T(4,128)}) custom-call(s32[16]{0:T(128)} %compare_select_fusion.1.first_ref, bf16[2176,3072]{1,0:T(8,128)(2,1)} %multiply_convert_fusion.q_ref.k_ref.v_ref, bf16[2176,3072]{1,0:T(8,128)(2,1)} %multiply_convert_fusion.q_ref.k_ref.v_ref, bf16[2176,3072]{1,0:T(8,128)(2,1)} %multiply_convert_fusion.q_ref.k_ref.v_ref), custom_call_target="tpu_custom_call" | custom-call | flops 18622709760 | bytes 8388608 | tf_op jit(solution)/shard_map/attend/pallas_call | solution.py:175
  236.4 19.4 %collective-permute-done.11 = bf16[1024,1024]{1,0:T(8,128)(2,1)S(1)} collective-permute-done((bf16[1024,1024]{1,0:T(8,128)(2,1)S(1)}, bf16[1024,1024]{1,0:T(8,128)(2,1)S(1)}, u32[]{:S(2)}, u32[]{:S(2)}) %collective-permute-start.11) | collective-permute-done | bytes 2097184 | tf_op jit(solution)/shard_map/ppermute | solution.py:358
  256.1 8.4 %multiply_convert_fusion.2 = (bf16[1024,2048]{1,0:T(8,128)(2,1)}, f32[1024,2048]{1,0:T(8,128)}) fusion(f32[2048]{0:T(1024)S(1)} %get-tuple-element.211, bf16[1024,1024]{1,0:T(8,128)(2,1)S(1)} %add_convert_fusion, bf16[2048,1024]{1,0:T(8,128)(2,1)S(1)} %pad_maximum_fusion), kind=kOutput, calls=%fused_computation.25 | convolution fusion | flops 4309647360 | bytes 18882560 | tf_op jit(solution)/shard_map/dot_general | solution.py:20
  264.5 7.7 %multiply_convert_fusion.1 = (bf16[1024,2048]{1,0:T(8,128)(2,1)S(1)}, f32[1024,2048]{1,0:T(8,128)}) fusion(f32[2048]{0:T(1024)S(1)} %get-tuple-element.210, bf16[1024,1024]{1,0:T(8,128)(2,1)S(1)} %add_convert_fusion, bf16[2048,1024]{1,0:T(8,128)(2,1)S(1)} %collective-permute-done.13), kind=kOutput, calls=%fused_computation.23 | convolution fusion | flops 4309647360 | bytes 18882560 | tf_op jit(solution)/shard_map/dot_general | solution.py:20
  279.2 11.7 %convert_reduce_fusion.1 = (f32[2048]{0:T(1024)}, bf16[1024,2048]{1,0:T(8,128)(2,1)S(1)}) fusion(f32[1024,2048]{1,0:T(8,128)} %get-tuple-element.223, f32[2048]{0:T(1024)S(1)} %get-tuple-element.210, bf16[2048,1024]{1,0:T(8,128)(2,1)} %collective-permute-done.12, bf16[1024,1024]{1,0:T(8,128)(2,1)S(1)} %copy-done.16, f32[1024]{0:T(1024)S(1)} %convert_element_type.191), kind=kOutput, calls=%fused_computation.19 | convolution fusion | flops 4329568256 | bytes 18894848 | tf_op jit(solution)/shard_map/dot_general | solution.py:20
  299.0 9.3 %fusion.13 = bf16[1024,2048]{1,0:T(8,128)(2,1)S(1)} fusion(f32[1024,2048]{1,0:T(8,128)} %get-tuple-element.221, f32[2048]{0:T(1024)S(1)} %get-tuple-element.211, bf16[2048,1024]{1,0:T(8,128)(2,1)S(1)} %copy-done.19, bf16[1024,1024]{1,0:T(8,128)(2,1)S(1)} %copy-done.16, f32[1024]{0:T(1024)S(1)} %convert_element_type.191), kind=kOutput, calls=%fused_computation.18 | convolution fusion | flops 4325376000 | bytes 18886656 | tf_op jit(solution)/shard_map/dot_general | solution.py:20
  308.3 7.1 %fusion.73 = f32[2048,1024]{1,0:T(8,128)} fusion(bf16[1024,2048]{1,0:T(8,128)(2,1)S(1)} %fusion.13, bf16[1024,1024]{1,0:T(8,128)(2,1)S(1)} %add_convert_fusion), kind=kOutput, calls=%fused_computation.213 | convolution fusion | flops 4294967296 | bytes 14680064 | tf_op jit(solution)/shard_map/dot_general | solution.py:24
  320.0 9.7 %multiply_convert_fusion.3 = bf16[1024,1024]{1,0:T(8,128)(2,1)} fusion(f32[1024,1024]{1,0:T(8,128)S(1)} %get-tuple-element.219, f32[1024,1024]{1,0:T(8,128)S(1)} %fusion.72, f32[1024]{0:T(1024)S(1)} %copy-done.55, f32[1024]{0:T(1024)S(1)} %convert_element_type.191, bf16[1024,2048]{1,0:T(8,128)(2,1)} %copy-done.69, ...), kind=kOutput, calls=%fused_computation.53 | convolution fusion | flops 4300210176 | bytes 18882560 | tf_op jit(solution)/shard_map/dot_general | solution.py:28
  329.7 10.1 %convert_add_fusion = f32[2048,1024]{1,0:T(8,128)S(1)} fusion(bf16[2048,1024]{1,0:T(8,128)(2,1)} %collective-permute-done.15, bf16[1024,2048]{1,0:T(8,128)(2,1)S(1)} %copy-done.68, bf16[1024,1024]{1,0:T(8,128)(2,1)S(1)} %copy-done.16, f32[1024]{0:T(1024)S(1)} %convert_element_type.191), kind=kOutput, calls=%fused_computation.21 | convolution fusion | flops 4302307328 | bytes 18878464 | tf_op jit(solution)/shard_map/dot_general | solution.py:24
  356.0 9.3 %fusion.74 = f32[1024,1024]{1,0:T(8,128)} fusion(bf16[1024,2048]{1,0:T(8,128)(2,1)S(1)} %copy-done.14, bf16[2048,1024]{1,0:T(8,128)(2,1)} %copy-done.15), kind=kOutput, calls=%fused_computation.214 | convolution fusion | flops 4294967296 | bytes 12582912 | tf_op jit(solution)/shard_map/dot_general | solution.py:28
  365.4 7.7 %multiply_reduce_fusion = (f32[1024]{0:T(1024)S(1)}, f32[1024]{0:T(1024)S(1)}, f32[1024]{0:T(1024)S(1)}, f32[1024]{0:T(1024)S(1)}, f32[1024,1024]{1,0:T(8,128)S(1)}) fusion(f32[1024,1024]{1,0:T(8,128)S(1)} %get-tuple-element.219, f32[1024]{0:T(1024)S(1)} %copy-done.44, f32[1024]{0:T(1024)S(1)} %copy-done.40, f32[1024]{0:T(1024)S(1)} %copy-done.42, ...), kind=kOutput, calls=%fused_computation.47 | convolution fusion | flops 4305448960 | bytes 21000192 | tf_op jit(solution)/shard_map/dot_general | solution.py:28
  389.2 13.5 %collective-permute-done.16 = bf16[1024,1024]{1,0:T(8,128)(2,1)} collective-permute-done((bf16[1024,1024]{1,0:T(8,128)(2,1)}, bf16[1024,1024]{1,0:T(8,128)(2,1)}, u32[]{:S(2)}, u32[]{:S(2)}) %collective-permute-start.16) | collective-permute-done | bytes 2097184 | tf_op jit(solution)/shard_map/ppermute | solution.py:358
  415.4 28.8 %attend_back.2.first_ref = bf16[2176,1536]{1,0:T(8,128)(2,1)} custom-call(s32[16]{0:T(128)} %compare_select_fusion.1.first_ref, bf16[2176,3072]{1,0:T(8,128)(2,1)} %multiply_convert_fusion.q_ref.k_ref.v_ref, bf16[2176,3072]{1,0:T(8,128)(2,1)} %multiply_convert_fusion.q_ref.k_ref.v_ref, bf16[2176,3072]{1,0:T(8,128)(2,1)} %multiply_convert_fusion.q_ref.k_ref.v_ref, ...), custom_call_target="tpu_custom_call" | custom-call | flops 31037849600 | bytes 8388608 | tf_op jit(solution)/shard_map/attend_back/pallas_call | solution.py:200
  457.1 6.8 convolution_convert_fusion.4
  464.0 8.4 %collective-permute-start.23 = (bf16[128,2048]{1,0:T(8,128)(2,1)S(1)}, bf16[128,2048]{1,0:T(8,128)(2,1)S(1)}, u32[]{:S(2)}, u32[]{:S(2)}) collective-permute-start(bf16[128,2048]{1,0:T(8,128)(2,1)S(1)} %pad_maximum_fusion.7), channel_id=1, source_target_pairs={{0,24},{1,25},{2,26},{3,27},{4,28},{5,29},{6,30},{7,31},{8,0},{9,1... | collective-permute-start | bytes 1572872 | tf_op jit(solution)/shard_map/ppermute | solution.py:358
  486.4 28.9 %attend_back.3.second_ref = bf16[2176,1536]{1,0:T(8,128)(2,1)} custom-call(s32[16]{0:T(128)} %compare_select_fusion.1.first_ref, bf16[2176,3072]{1,0:T(8,128)(2,1)} %multiply_convert_fusion.q_ref.k_ref.v_ref, bf16[2176,3072]{1,0:T(8,128)(2,1)} %multiply_convert_fusion.q_ref.k_ref.v_ref, bf16[2176,3072]{1,0:T(8,128)(2,1)} %multiply_convert_fusion.q_ref.k_ref.v_ref, ...), custom_call_target="tpu_custom_call" | custom-call | flops 31037849600 | bytes 8388608 | tf_op jit(solution)/shard_map/attend_back/pallas_call | solution.py:200
  515.3 13.0 %collective-permute-done.22 = bf16[128,2048]{1,0:T(8,128)(2,1)S(1)} collective-permute-done((bf16[128,2048]{1,0:T(8,128)(2,1)S(1)}, bf16[128,2048]{1,0:T(8,128)(2,1)S(1)}, u32[]{:S(2)}, u32[]{:S(2)}) %collective-permute-start.22) | collective-permute-done | bytes 524320 | tf_op jit(solution)/shard_map/ppermute | solution.py:358
  569.9 22.7 %into_norm.1 = (bf16[2176,1024]{1,0:T(8,128)(2,1)}, f32[2,1024]{1,0:T(2,128)}, f32[1,3072]{1,0:T(1,128)}) custom-call(bf16[2176,1536]{1,0:T(8,128)(2,1)} %attend_back.2.first_ref, bf16[2176,1536]{1,0:T(8,128)(2,1)} %attend_back.3.second_ref, bf16[1024,3200]{1,0:T(8,128)(2,1)} %all-gather.5.cloned.1.call-done.w_ref, bf16[2176,1024]{1,0:T(8,128)(2,1)} %copy-done.3), custom_call_target="tpu_custom_call" | custom-call | flops 13690208256 | bytes 26738688 | tf_op jit(solution)/shard_map/into_norm/pallas_call | solution.py:251
  642.4 10.7 %collective-permute-done.32 = bf16[32,1536]{1,0:T(8,128)(2,1)S(1)} collective-permute-done((bf16[32,1536]{1,0:T(8,128)(2,1)S(1)}, bf16[32,1536]{1,0:T(8,128)(2,1)S(1)}, u32[]{:S(2)}, u32[]{:S(2)}) %collective-permute-start.32) | collective-permute-done | bytes 98336 | tf_op jit(solution)/shard_map/ppermute | solution.py:358
  668.8 15.1 %all-gather.9.cloned.1.call-done = f32[32,1,12288]{2,1,0:T(1,128)} async-done(((f32[1,1,12288]{2,1,0:T(1,128)}), f32[32,1,12288]{2,1,0:T(1,128)}) %all-gather.9.cloned.1.call-update) | async-done | bytes 1572880 | tf_op jit(solution)/shard_map/all_gather | solution.py:647
  (398 shorter events, 284.2 us)
Async XLA Ops:
  7.2 93.4 %all-gather.5.cloned.1.call-start = ((), (), s32[]{:S(2)}) async-start(), calls=%async_computation.1 | async-start | bytes 6758400 | tf_op jit(solution)/shard_map/all_gather | solution.py:452
  22.2 165.9 %all-gather.7.cloned.1.call-start = ((), (), s32[]{:S(2)}) async-start(), calls=%async_computation.2 | async-start | bytes 2162688 | tf_op jit(solution)/shard_map/all_gather | solution.py:455
  30.3 593.3 %reduce-scatter.2.cloned.1.call-start = ((), (), s32[]{:S(2)}) async-start(), calls=%async_computation.3 | async-start | bytes 4325376 | tf_op jit(solution)/shard_map/reduce_scatter | solution.py:562
  104.5 49.4 %collective-permute-start.3 = (bf16[128,1024]{1,0:T(8,128)(2,1)S(1)}, bf16[128,1024]{1,0:T(8,128)(2,1)}, u32[]{:S(2)}, u32[]{:S(2)}) collective-permute-start(bf16[128,1024]{1,0:T(8,128)(2,1)S(1)} %copy-done.32), channel_id=1, source_target_pairs={{0,16},{1,17},{2,18},{3,19},{4,20},{5,21},{6,22},{7,23},{8,24},{9,... | collective-permute-start | bytes 786440 | tf_op jit(solution)/shard_map/ppermute | solution.py:358
  105.6 48.2 %collective-permute-start.4 = (bf16[128,1024]{1,0:T(8,128)(2,1)S(1)}, bf16[128,1024]{1,0:T(8,128)(2,1)}, u32[]{:S(2)}, u32[]{:S(2)}) collective-permute-start(bf16[128,1024]{1,0:T(8,128)(2,1)S(1)} %copy-done.32), channel_id=1, source_target_pairs={{0,8},{1,9},{2,10},{3,11},{4,12},{5,13},{6,14},{7,15},{8,16},{9,17... | collective-permute-start | bytes 786440 | tf_op jit(solution)/shard_map/ppermute | solution.py:358
  106.5 50.8 %collective-permute-start.6 = (bf16[128,1024]{1,0:T(8,128)(2,1)}, bf16[128,1024]{1,0:T(8,128)(2,1)S(1)}, u32[]{:S(2)}, u32[]{:S(2)}) collective-permute-start(bf16[128,1024]{1,0:T(8,128)(2,1)} %param.34), channel_id=1, source_target_pairs={{0,24},{1,25},{2,26},{3,27},{4,28},{5,29},{6,30},{7,31},{8,0},{9,1... | collective-permute-start | bytes 786440 | tf_op jit(solution)/shard_map/ppermute | solution.py:358
  109.4 47.8 %collective-permute-start.7 = (bf16[128,1024]{1,0:T(8,128)(2,1)}, bf16[128,1024]{1,0:T(8,128)(2,1)S(1)}, u32[]{:S(2)}, u32[]{:S(2)}) collective-permute-start(bf16[128,1024]{1,0:T(8,128)(2,1)} %param.34), channel_id=1, source_target_pairs={{0,16},{1,17},{2,18},{3,19},{4,20},{5,21},{6,22},{7,23},{8,24},{9,... | collective-permute-start | bytes 786440 | tf_op jit(solution)/shard_map/ppermute | solution.py:358
  188.1 37.6 %collective-permute-start.9 = (bf16[1024,1024]{1,0:T(8,128)(2,1)}, bf16[1024,1024]{1,0:T(8,128)(2,1)}, u32[]{:S(2)}, u32[]{:S(2)}) collective-permute-start(bf16[1024,1024]{1,0:T(8,128)(2,1)} %pad_maximum_fusion.1), channel_id=1, source_target_pairs={{0,4},{1,3},{2,6},{3,1},{4,0},{5,7},{6,2},{7,5},{8,12},{9,11},{10,... | collective-permute-start | bytes 6291464 | tf_op jit(solution)/shard_map/ppermute | solution.py:358
  229.5 35.0 %collective-permute-start.13 = (bf16[2048,1024]{1,0:T(8,128)(2,1)S(1)}, bf16[2048,1024]{1,0:T(8,128)(2,1)S(1)}, u32[]{:S(2)}, u32[]{:S(2)}) collective-permute-start(bf16[2048,1024]{1,0:T(8,128)(2,1)S(1)} %pad_maximum_fusion), channel_id=1, source_target_pairs={{0,1},{1,0},{2,3},{3,2},{4,5},{5,4},{6,7},{7,6},{8,9},{9,8},{10,11... | collective-permute-start | bytes 12582920 | tf_op jit(solution)/shard_map/ppermute | solution.py:358
  278.7 51.0 %collective-permute-start.15 = (bf16[2048,1024]{1,0:T(8,128)(2,1)}, bf16[2048,1024]{1,0:T(8,128)(2,1)}, u32[]{:S(2)}, u32[]{:S(2)}) collective-permute-start(bf16[2048,1024]{1,0:T(8,128)(2,1)} %convolution_convert_fusion.1), channel_id=1, source_target_pairs={{0,1},{1,0},{2,3},{3,2},{4,5},{5,4},{6,7},{7,6},{8,9},{9,8},{10,11... | collective-permute-start | bytes 12582920 | tf_op jit(solution)/shard_map/ppermute | solution.py:358
  299.0 30.8 %collective-permute-start.14 = (bf16[2048,1024]{1,0:T(8,128)(2,1)}, bf16[2048,1024]{1,0:T(8,128)(2,1)S(1)}, u32[]{:S(2)}, u32[]{:S(2)}) collective-permute-start(bf16[2048,1024]{1,0:T(8,128)(2,1)} %convolution_convert_fusion.2), channel_id=1, source_target_pairs={{0,1},{1,0},{2,3},{3,2},{4,5},{5,4},{6,7},{7,6},{8,9},{9,8},{10,11... | collective-permute-start | bytes 12582920 | tf_op jit(solution)/shard_map/ppermute | solution.py:358
  352.4 36.8 %collective-permute-start.17 = (bf16[1024,1024]{1,0:T(8,128)(2,1)}, bf16[1024,1024]{1,0:T(8,128)(2,1)}, u32[]{:S(2)}, u32[]{:S(2)}) collective-permute-start(bf16[1024,1024]{1,0:T(8,128)(2,1)} %slice.672), channel_id=1, source_target_pairs={{0,4},{1,3},{2,6},{3,1},{4,0},{5,7},{6,2},{7,5},{8,12},{9,11},{10,... | collective-permute-start | bytes 6291464 | tf_op jit(solution)/shard_map/ppermute | solution.py:358
  352.5 50.2 %collective-permute-start.16 = (bf16[1024,1024]{1,0:T(8,128)(2,1)}, bf16[1024,1024]{1,0:T(8,128)(2,1)}, u32[]{:S(2)}, u32[]{:S(2)}) collective-permute-start(bf16[1024,1024]{1,0:T(8,128)(2,1)} %slice.673), channel_id=1, source_target_pairs={{0,4},{1,3},{2,6},{3,1},{4,0},{5,7},{6,2},{7,5},{8,12},{9,11},{10,... | collective-permute-start | bytes 6291464 | tf_op jit(solution)/shard_map/ppermute | solution.py:358
  381.7 302.1 %all-gather.9.cloned.1.call-start = ((), (), s32[]{:S(2)}) async-start(), calls=%async_computation.4 | async-start | bytes 1622016 | tf_op jit(solution)/shard_map/all_gather | solution.py:647
  413.3 30.8 %collective-permute-start.19 = (bf16[512,1024]{1,0:T(8,128)(2,1)S(1)}, bf16[512,1024]{1,0:T(8,128)(2,1)S(1)}, u32[]{:S(2)}, u32[]{:S(2)}) collective-permute-start(bf16[512,1024]{1,0:T(8,128)(2,1)S(1)} %slice.674), channel_id=1, source_target_pairs={{0,2},{1,5},{2,0},{3,7},{4,6},{5,1},{6,4},{7,3},{8,10},{9,13},{10,... | collective-permute-start | bytes 3145736 | tf_op jit(solution)/shard_map/ppermute | solution.py:358
  413.3 36.2 %collective-permute-start.18 = (bf16[512,1024]{1,0:T(8,128)(2,1)S(1)}, bf16[512,1024]{1,0:T(8,128)(2,1)}, u32[]{:S(2)}, u32[]{:S(2)}) collective-permute-start(bf16[512,1024]{1,0:T(8,128)(2,1)S(1)} %slice.675), channel_id=1, source_target_pairs={{0,2},{1,5},{2,0},{3,7},{4,6},{5,1},{6,4},{7,3},{8,10},{9,13},{10,... | collective-permute-start | bytes 3145736 | tf_op jit(solution)/shard_map/ppermute | solution.py:358
  464.0 65.9 %collective-permute-start.20 = (bf16[512,1536]{1,0:T(8,128)(2,1)}, bf16[512,1536]{1,0:T(8,128)(2,1)}, u32[]{:S(2)}, u32[]{:S(2)}) collective-permute-start(bf16[512,1536]{1,0:T(8,128)(2,1)} %convolution_convert_fusion.4), channel_id=1, source_target_pairs={{0,1},{1,0},{2,3},{3,2},{4,5},{5,4},{6,7},{7,6},{8,9},{9,8},{10,11... | collective-permute-start | bytes 4718600 | tf_op jit(solution)/shard_map/ppermute | solution.py:358
  464.0 51.3 %collective-permute-start.23 = (bf16[128,2048]{1,0:T(8,128)(2,1)S(1)}, bf16[128,2048]{1,0:T(8,128)(2,1)S(1)}, u32[]{:S(2)}, u32[]{:S(2)}) collective-permute-start(bf16[128,2048]{1,0:T(8,128)(2,1)S(1)} %pad_maximum_fusion.7), channel_id=1, source_target_pairs={{0,24},{1,25},{2,26},{3,27},{4,28},{5,29},{6,30},{7,31},{8,0},{9,1... | collective-permute-start | bytes 1572872 | tf_op jit(solution)/shard_map/ppermute | solution.py:358
  472.4 55.9 %collective-permute-start.22 = (bf16[128,2048]{1,0:T(8,128)(2,1)S(1)}, bf16[128,2048]{1,0:T(8,128)(2,1)S(1)}, u32[]{:S(2)}, u32[]{:S(2)}) collective-permute-start(bf16[128,2048]{1,0:T(8,128)(2,1)S(1)} %pad_maximum_fusion.6), channel_id=1, source_target_pairs={{0,16},{1,17},{2,18},{3,19},{4,20},{5,21},{6,22},{7,23},{8,24},{9,... | collective-permute-start | bytes 1572872 | tf_op jit(solution)/shard_map/ppermute | solution.py:358
  478.7 49.6 %collective-permute-start.21 = (bf16[128,2048]{1,0:T(8,128)(2,1)S(1)}, bf16[128,2048]{1,0:T(8,128)(2,1)S(1)}, u32[]{:S(2)}, u32[]{:S(2)}) collective-permute-start(bf16[128,2048]{1,0:T(8,128)(2,1)S(1)} %pad_maximum_fusion.5), channel_id=1, source_target_pairs={{0,8},{1,9},{2,10},{3,11},{4,12},{5,13},{6,14},{7,15},{8,16},{9,17... | collective-permute-start | bytes 1572872 | tf_op jit(solution)/shard_map/ppermute | solution.py:358
  563.7 59.8 %collective-permute-start.26 = (bf16[128,1536]{1,0:T(8,128)(2,1)}, bf16[128,1536]{1,0:T(8,128)(2,1)S(1)}, u32[]{:S(2)}, u32[]{:S(2)}) collective-permute-start(bf16[128,1536]{1,0:T(8,128)(2,1)} %slice.679), channel_id=1, source_target_pairs={{0,2},{1,5},{2,0},{3,7},{4,6},{5,1},{6,4},{7,3},{8,10},{9,13},{10,... | collective-permute-start | bytes 1179656 | tf_op jit(solution)/shard_map/ppermute | solution.py:358
  567.9 55.6 %collective-permute-start.27 = (bf16[256,1536]{1,0:T(8,128)(2,1)}, bf16[256,1536]{1,0:T(8,128)(2,1)}, u32[]{:S(2)}, u32[]{:S(2)}) collective-permute-start(bf16[256,1536]{1,0:T(8,128)(2,1)} %slice.676), channel_id=1, source_target_pairs={{0,4},{1,3},{2,6},{3,1},{4,0},{5,7},{6,2},{7,5},{8,12},{9,11},{10,... | collective-permute-start | bytes 2359304 | tf_op jit(solution)/shard_map/ppermute | solution.py:358
  619.9 39.8 %collective-permute-start.29 = (bf16[576,1024]{1,0:T(8,128)(2,1)}, bf16[576,1024]{1,0:T(8,128)(2,1)}, u32[]{:S(2)}, u32[]{:S(2)}) collective-permute-start(bf16[576,1024]{1,0:T(8,128)(2,1)} %get-tuple-element.177), channel_id=1, source_target_pairs={{0,1},{1,2},{2,3},{3,4},{4,5},{5,6},{6,7},{7,8},{8,9},{9,10},{10,1... | collective-permute-start | bytes 3538952 | tf_op jit(solution)/shard_map/ppermute | solution.py:332
  622.2 37.5 %collective-permute-start.30 = (bf16[576,1024]{1,0:T(8,128)(2,1)}, bf16[576,1024]{1,0:T(8,128)(2,1)}, u32[]{:S(2)}, u32[]{:S(2)}) collective-permute-start(bf16[576,1024]{1,0:T(8,128)(2,1)} %get-tuple-element.178), channel_id=1, source_target_pairs={{1,0},{2,1},{3,2},{4,3},{5,4},{6,5},{7,6},{8,7},{9,8},{10,9},{11,1... | collective-permute-start | bytes 3538952 | tf_op jit(solution)/shard_map/ppermute | solution.py:332
  (91 other events, 1404.4 us)
Sparse Core Ops, SparseCore 0:
  22.3 78.2 all-gather.4
  103.5 71.1 all-gather.6
  381.8 151.2 reduce-scatter.1
  623.6 60.1 all-gather.8
